TPU v7x, 768 devices: a whole 4x8x12 slice. The times are simulated.
768 devices in a mesh: group: 96 (over x, z, core), sub: 8 (over y).
Axes of the slice: x: 4, y: 8, z: 12, core: 2. Of those that a mesh axis runs over, the one named last changes fastest.
Arguments:
- fields: float32 [4, 84, 98304], P(None, None, ('group', 'sub')), may hold values from -6 to 6
- diff_ops: float32 [3, 84, 84], replicated, may hold values from -0.625 to 0.625
- face_interp: float32 [112, 84], replicated, may hold values from -0.625 to 0.625
- lift: float32 [84, 112], replicated, may hold values from -0.5 to 0.5
- inv_jacobian: float32 [3, 3, 98304], P(None, None, ('group', 'sub')), may hold values from -4 to 4
- face_scale: float32 [4, 98304], P(None, ('group', 'sub')), may hold values from 1 to 4
- normal_angle: float32 [2, 4, 98304], P(None, None, ('group', 'sub')), may hold values from -3.140625 to 3.140625
- reflect: float32 [4], replicated, may hold values from -0.5 to 1
- send_list: int32 [4, 12288], P(None, ('group', 'sub')), may hold values from 0 to 511, as said below
- recv_map: int32 [4, 98304], P(None, ('group', 'sub')), may hold values from 0 to 575, as said below
- face_class: int32 [4, 98304], P(None, ('group', 'sub')), may hold values from 0 to 4
Outputs:
- pressure_velocity: float32 [4, 84, 98304], P(None, None, ('group', 'sub'))
Inputs may be any that keep to these rules, and one draw needn't show every extreme that they name: `recv_map`: values below 512 name a local face of the same device; 512 + j * 16 + s names slot s of the buffer received from neighbour j (0 previous sub, 1 next sub, 2 previous group, 3 next group). Only read where face_class is 0; the used slots from each neighbour form a prefix, and no slot of a missing device is named. `send_list`: local face ids, distinct within a device.
All inputs are finite; a program needn't handle non-finite values.
Results may differ from a plain program's by a relative error of at most 0.0003.
Values sent between devices are 32-bit elements; how exact they have to be, the bound alone decides.
A program may use at most 32 MiB of HBM per device.

v0:
```python
import jax
import jax.numpy as jnp
from jax import lax
from jax.sharding import PartitionSpec as P

SECTIONS = 5


RK_A = (
    0.0,
    -567301805773.0 / 1357537059087.0,
    -2404267990393.0 / 2016746695238.0,
    -3550918686646.0 / 2091501179385.0,
    -1275806237668.0 / 842570457699.0,
)
RK_B = (
    1432997174477.0 / 9575080441755.0,
    5161836677717.0 / 13612068292357.0,
    1720146321549.0 / 2090206949498.0,
    3134564353537.0 / 4481467310338.0,
    2277821191437.0 / 14882151754819.0,
)
DT = 0.3
HIGH = lax.Precision.HIGHEST


def extended(block, sides, width):
    for axis, dim in sides:
        count = lax.axis_size(axis)
        forward = [(i, i + 1) for i in range(count - 1)]
        backward = [(target, source) for source, target in forward]
        low = lax.ppermute(
            lax.slice_in_dim(block, block.shape[dim] - width, None, axis=dim), axis, forward
        )
        high = lax.ppermute(lax.slice_in_dim(block, 0, width, axis=dim), axis, backward)
        block = jnp.concatenate([low, block, high], axis=dim)
    return block


def face_traces(state_now, face_interp, face_count):
    traces = jnp.einsum("jn,fne->fje", face_interp, state_now, precision=HIGH)
    nfield, trace_rows, elem_count = traces.shape
    per_face = traces.reshape(nfield, face_count, trace_rows // face_count, elem_count).transpose(
        0, 2, 1, 3
    )
    return per_face.reshape(nfield, trace_rows // face_count, face_count * elem_count)


def unit_normals(angles):
    first, second = (angles[0], angles[1])
    return jnp.stack(
        [jnp.cos(first) * jnp.cos(second), jnp.sin(first) * jnp.cos(second), jnp.sin(second)]
    )


def face_reflect(face_class, reflect):
    classes = jnp.arange(1, reflect.shape[0] + 1, dtype=jnp.int32)
    return jnp.sum(
        jnp.where(face_class[None] == classes[:, None, None], reflect[:, None, None], 0.0), axis=0
    )


def tendency(
    state_now,
    own_trace,
    neighbour,
    diff_ops,
    lift,
    inv_jacobian,
    face_scale,
    normal_dirs,
    interior,
    reflect_face,
):
    face_count = face_scale.shape[0]
    elem_count = state_now.shape[2]
    normal_rows = normal_dirs.reshape(3, 1, -1)
    un_own = jnp.sum(normal_rows * own_trace[1:4], axis=0)
    un_nbr = jnp.sum(normal_rows * neighbour[1:4], axis=0)
    jump_term = 0.5 * (neighbour[0] - un_nbr - (own_trace[0] - un_own))
    wall_term = 0.5 * (
        reflect_face.reshape(1, -1) * (own_trace[0] + un_own) - (own_trace[0] - un_own)
    )
    upwind = jnp.where(interior.reshape(1, -1), jump_term, wall_term) * face_scale.reshape(1, -1)
    flux_terms = jnp.concatenate([upwind[None], -normal_rows * upwind[None]], axis=0)
    face_rows = flux_terms.shape[1]
    flux_terms = (
        flux_terms.reshape(4, face_rows, face_count, elem_count)
        .transpose(0, 2, 1, 3)
        .reshape(4, face_count * face_rows, elem_count)
    )
    lifted = jnp.einsum("nj,fje->fne", lift, flux_terms, precision=HIGH)
    slopes = jnp.einsum("anm,fme->afne", diff_ops, state_now, precision=HIGH)
    grad_p = jnp.einsum("ace,ane->cne", inv_jacobian, slopes[:, 0], precision=HIGH)
    diverg = jnp.einsum("ace,acne->ne", inv_jacobian, slopes[:, 1:4], precision=HIGH)
    return jnp.concatenate([-diverg[None], -grad_p], axis=0) + lifted


def shards(
    fields,
    diff_ops,
    face_interp,
    lift,
    inv_jacobian,
    face_scale,
    normal_angle,
    reflect,
    send_list,
    recv_map,
    face_class,
):
    face_count = face_scale.shape[0]
    normal_dirs = unit_normals(normal_angle).reshape(3, -1)
    interior = (face_class == 0).reshape(-1)
    reflect_face = face_reflect(face_class, reflect).reshape(-1)
    lookup = recv_map.reshape(-1)
    residue = jnp.zeros_like(fields)
    current = fields
    for section_index in range(SECTIONS):
        own_trace = face_traces(current, face_interp, face_count)
        packed = jnp.moveaxis(jnp.take(own_trace, send_list, axis=2), 2, 0)
        along_sub = extended(jnp.stack([packed[1], packed[0]]), (("sub", 0),), 1)
        along_group = extended(jnp.stack([packed[3], packed[2]]), (("group", 0),), 1)
        arrived = [along_sub[0], along_sub[3], along_group[0], along_group[3]]
        source_table = jnp.concatenate([own_trace] + arrived, axis=2)
        neighbour = jnp.take(source_table, lookup, axis=2)
        change = tendency(
            current,
            own_trace,
            neighbour,
            diff_ops,
            lift,
            inv_jacobian,
            face_scale,
            normal_dirs,
            interior,
            reflect_face,
        )
        residue = RK_A[section_index] * residue + DT * change
        current = current + RK_B[section_index] * residue
    return current


def solution(mesh):
    return jax.shard_map(
        shards,
        mesh=mesh,
        in_specs=(
            P(None, None, ("group", "sub")),
            P(),
            P(),
            P(),
            P(None, None, ("group", "sub")),
            P(None, ("group", "sub")),
            P(None, None, ("group", "sub")),
            P(),
            P(None, ("group", "sub")),
            P(None, ("group", "sub")),
            P(None, ("group", "sub")),
        ),
        out_specs=P(None, None, ("group", "sub")),
        check_vma=False,
    )
```

profile of v0, /device:TPU:38, one launch (start us, length us, event | category | flops | bytes accessed | tf_op | source)
XLA Modules:
  0.0 140.6 jit_solution(16360180825314618191)
XLA Ops:
  0.0 0.7 compare_select_fusion.1
  0.7 0.7 compare_and_fusion.1
  1.4 1.3 convolution_bitcast_fusion.9
  3.4 0.7 gather_fusion
  4.9 2.6 %collective-permute-start = (f32[1,4,28,16]{2,1,3,0:T(4,128)}, f32[1,4,28,16]{2,1,3,0:T(4,128)}, u32[]{:S(2)}, u32[]{:S(2)}) collective-permute-start(f32[1,4,28,16]{2,1,3,0:T(4,128)} %get-tuple-element.32), channel_id=1, source_target_pairs={{0,1},{1,2},{2,3},{3,4},{4,5},{5,6},{6,7},{8,9},{9,10},{10,11},{11... | collective-permute-start | bytes 21512 | tf_op jit(solution)/shard_map/ppermute | solution.py:32
  7.5 4.5 %collective-permute-start.1 = (f32[1,4,28,16]{2,1,3,0:T(4,128)}, f32[1,4,28,16]{2,1,3,0:T(4,128)}, u32[]{:S(2)}, u32[]{:S(2)}) collective-permute-start(f32[1,4,28,16]{2,1,3,0:T(4,128)} %get-tuple-element.31), channel_id=1, source_target_pairs={{1,0},{2,1},{3,2},{4,3},{5,4},{6,5},{7,6},{9,8},{10,9},{11,10},{12... | collective-permute-start | bytes 21512 | tf_op jit(solution)/shard_map/ppermute | solution.py:35
  11.9 1.9 %collective-permute-start.2 = (f32[1,4,28,16]{2,1,3,0:T(4,128)}, f32[1,4,28,16]{2,1,3,0:T(4,128)}, u32[]{:S(2)}, u32[]{:S(2)}) collective-permute-start(f32[1,4,28,16]{2,1,3,0:T(4,128)} %get-tuple-element.30), channel_id=1, source_target_pairs={{0,8},{8,16},{16,24},{24,32},{32,40},{40,48},{48,56},{56,64},{64,7... | collective-permute-start | bytes 21512 | tf_op jit(solution)/shard_map/ppermute | solution.py:32
  13.9 13.9 %collective-permute-start.3 = (f32[1,4,28,16]{2,1,3,0:T(4,128)}, f32[1,4,28,16]{2,1,3,0:T(4,128)}, u32[]{:S(2)}, u32[]{:S(2)}) collective-permute-start(f32[1,4,28,16]{2,1,3,0:T(4,128)} %get-tuple-element.29), channel_id=1, source_target_pairs={{8,0},{16,8},{24,16},{32,24},{40,32},{48,40},{56,48},{64,56},{72,6... | collective-permute-start | bytes 21512 | tf_op jit(solution)/shard_map/ppermute | solution.py:35
  30.3 1.0 fusion.84
  31.8 0.7 copy.410
  32.5 0.8 constant_dynamic-update-slice_fusion.3
  33.3 0.8 constant_dynamic-update-slice_fusion.2
  34.1 0.8 constant_dynamic-update-slice_fusion.1
  34.9 0.8 constant_dynamic-update-slice_fusion
  35.6 2.1 %gather_fusion.1 = f32[512,4,28]{2,1,0:T(4,128)S(1)} fusion(f32[4,28,576]{1,0,2:T(4,128)S(1)} %constant_dynamic-update-slice_fusion, s32[1024]{0:T(1024)S(1)} %pad_clamp_fusion), kind=kCustom, calls=%fused_computation.1.clone | custom fusion | bytes 460800 | tf_op jit(solution)/shard_map/jit(_take)/gather | solution.py:126
  39.9 0.7 slice.266
  41.8 0.7 gather_fusion.2
  44.0 0.7 copy.431
  44.8 1.9 %collective-permute-start.4 = (f32[1,4,28,16]{2,1,3,0:T(4,128)S(1)}, f32[1,4,28,16]{2,1,3,0:T(4,128)S(1)}, u32[]{:S(2)}, u32[]{:S(2)}) collective-permute-start(f32[1,4,28,16]{2,1,3,0:T(4,128)S(1)} %get-tuple-element.28), channel_id=1, source_target_pairs={{0,1},{1,2},{2,3},{3,4},{4,5},{5,6},{6,7},{8,9},{9,10},{10,11},{11... | collective-permute-start | bytes 21512 | tf_op jit(solution)/shard_map/ppermute | solution.py:32
  46.7 5.1 %collective-permute-start.5 = (f32[1,4,28,16]{2,1,3,0:T(4,128)S(1)}, f32[1,4,28,16]{2,1,3,0:T(4,128)S(1)}, u32[]{:S(2)}, u32[]{:S(2)}) collective-permute-start(f32[1,4,28,16]{2,1,3,0:T(4,128)S(1)} %get-tuple-element.27), channel_id=1, source_target_pairs={{1,0},{2,1},{3,2},{4,3},{5,4},{6,5},{7,6},{9,8},{10,9},{11,10},{12... | collective-permute-start | bytes 21512 | tf_op jit(solution)/shard_map/ppermute | solution.py:35
  51.9 1.9 %collective-permute-start.6 = (f32[1,4,28,16]{2,1,3,0:T(4,128)S(1)}, f32[1,4,28,16]{2,1,3,0:T(4,128)S(1)}, u32[]{:S(2)}, u32[]{:S(2)}) collective-permute-start(f32[1,4,28,16]{2,1,3,0:T(4,128)S(1)} %get-tuple-element.26), channel_id=1, source_target_pairs={{0,8},{8,16},{16,24},{24,32},{32,40},{40,48},{48,56},{56,64},{64,7... | collective-permute-start | bytes 21512 | tf_op jit(solution)/shard_map/ppermute | solution.py:32
  53.8 5.9 %collective-permute-start.7 = (f32[1,4,28,16]{2,1,3,0:T(4,128)S(1)}, f32[1,4,28,16]{2,1,3,0:T(4,128)S(1)}, u32[]{:S(2)}, u32[]{:S(2)}) collective-permute-start(f32[1,4,28,16]{2,1,3,0:T(4,128)S(1)} %get-tuple-element.25), channel_id=1, source_target_pairs={{8,0},{16,8},{24,16},{32,24},{40,32},{48,40},{56,48},{64,56},{72,6... | collective-permute-start | bytes 21512 | tf_op jit(solution)/shard_map/ppermute | solution.py:35
  59.9 1.0 fusion.85
  61.0 0.7 negate_bitcast_fusion.3
  62.5 2.1 %gather_fusion.3 = f32[512,4,28]{2,1,0:T(4,128)S(1)} fusion(f32[4,28,576]{1,0,2:T(4,128)S(1)} %constant_dynamic-update-slice_fusion.5, s32[1024]{0:T(1024)S(1)} %copy-done.28), kind=kCustom, calls=%fused_computation.6.clone | custom fusion | bytes 460800 | tf_op jit(solution)/shard_map/jit(_take)/gather | solution.py:126
  69.5 0.7 copy.451
  70.4 1.9 %collective-permute-start.8 = (f32[1,4,28,16]{2,1,3,0:T(4,128)S(1)}, f32[1,4,28,16]{2,1,3,0:T(4,128)S(1)}, u32[]{:S(2)}, u32[]{:S(2)}) collective-permute-start(f32[1,4,28,16]{2,1,3,0:T(4,128)S(1)} %get-tuple-element.24), channel_id=1, source_target_pairs={{0,1},{1,2},{2,3},{3,4},{4,5},{5,6},{6,7},{8,9},{9,10},{10,11},{11... | collective-permute-start | bytes 21512 | tf_op jit(solution)/shard_map/ppermute | solution.py:32
  72.3 5.1 %collective-permute-start.9 = (f32[1,4,28,16]{2,1,3,0:T(4,128)S(1)}, f32[1,4,28,16]{2,1,3,0:T(4,128)S(1)}, u32[]{:S(2)}, u32[]{:S(2)}) collective-permute-start(f32[1,4,28,16]{2,1,3,0:T(4,128)S(1)} %get-tuple-element.23), channel_id=1, source_target_pairs={{1,0},{2,1},{3,2},{4,3},{5,4},{6,5},{7,6},{9,8},{10,9},{11,10},{12... | collective-permute-start | bytes 21512 | tf_op jit(solution)/shard_map/ppermute | solution.py:35
  77.4 1.9 %collective-permute-start.10 = (f32[1,4,28,16]{2,1,3,0:T(4,128)S(1)}, f32[1,4,28,16]{2,1,3,0:T(4,128)S(1)}, u32[]{:S(2)}, u32[]{:S(2)}) collective-permute-start(f32[1,4,28,16]{2,1,3,0:T(4,128)S(1)} %get-tuple-element.22), channel_id=1, source_target_pairs={{0,8},{8,16},{16,24},{24,32},{32,40},{40,48},{48,56},{56,64},{64,7... | collective-permute-start | bytes 21512 | tf_op jit(solution)/shard_map/ppermute | solution.py:32
  79.4 5.8 %collective-permute-start.11 = (f32[1,4,28,16]{2,1,3,0:T(4,128)S(1)}, f32[1,4,28,16]{2,1,3,0:T(4,128)S(1)}, u32[]{:S(2)}, u32[]{:S(2)}) collective-permute-start(f32[1,4,28,16]{2,1,3,0:T(4,128)S(1)} %get-tuple-element.21), channel_id=1, source_target_pairs={{8,0},{16,8},{24,16},{32,24},{40,32},{48,40},{56,48},{64,56},{72,6... | collective-permute-start | bytes 21512 | tf_op jit(solution)/shard_map/ppermute | solution.py:35
  85.3 1.0 fusion.86
  86.7 2.1 %gather_fusion.5 = f32[512,4,28]{2,1,0:T(4,128)S(1)} fusion(f32[4,28,576]{1,0,2:T(4,128)S(1)} %constant_dynamic-update-slice_fusion.10, s32[1024]{0:T(1024)S(1)} %copy-done.29), kind=kCustom, calls=%fused_computation.7.clone | custom fusion | bytes 460800 | tf_op jit(solution)/shard_map/jit(_take)/gather | solution.py:126
  90.4 0.9 multiply_add_fusion.1
  92.5 0.7 gather_fusion.6
  94.1 1.9 %collective-permute-start.12 = (f32[1,4,28,16]{2,1,3,0:T(4,128)S(1)}, f32[1,4,28,16]{2,1,3,0:T(4,128)S(1)}, u32[]{:S(2)}, u32[]{:S(2)}) collective-permute-start(f32[1,4,28,16]{2,1,3,0:T(4,128)S(1)} %get-tuple-element.20), channel_id=1, source_target_pairs={{0,1},{1,2},{2,3},{3,4},{4,5},{5,6},{6,7},{8,9},{9,10},{10,11},{11... | collective-permute-start | bytes 21512 | tf_op jit(solution)/shard_map/ppermute | solution.py:32
  96.0 5.1 %collective-permute-start.13 = (f32[1,4,28,16]{2,1,3,0:T(4,128)S(1)}, f32[1,4,28,16]{2,1,3,0:T(4,128)S(1)}, u32[]{:S(2)}, u32[]{:S(2)}) collective-permute-start(f32[1,4,28,16]{2,1,3,0:T(4,128)S(1)} %get-tuple-element.19), channel_id=1, source_target_pairs={{1,0},{2,1},{3,2},{4,3},{5,4},{6,5},{7,6},{9,8},{10,9},{11,10},{12... | collective-permute-start | bytes 21512 | tf_op jit(solution)/shard_map/ppermute | solution.py:35
  101.2 1.9 %collective-permute-start.14 = (f32[1,4,28,16]{2,1,3,0:T(4,128)S(1)}, f32[1,4,28,16]{2,1,3,0:T(4,128)S(1)}, u32[]{:S(2)}, u32[]{:S(2)}) collective-permute-start(f32[1,4,28,16]{2,1,3,0:T(4,128)S(1)} %get-tuple-element.18), channel_id=1, source_target_pairs={{0,8},{8,16},{16,24},{24,32},{32,40},{40,48},{48,56},{56,64},{64,7... | collective-permute-start | bytes 21512 | tf_op jit(solution)/shard_map/ppermute | solution.py:32
  103.1 6.0 %collective-permute-start.15 = (f32[1,4,28,16]{2,1,3,0:T(4,128)S(1)}, f32[1,4,28,16]{2,1,3,0:T(4,128)S(1)}, u32[]{:S(2)}, u32[]{:S(2)}) collective-permute-start(f32[1,4,28,16]{2,1,3,0:T(4,128)S(1)} %get-tuple-element.17), channel_id=1, source_target_pairs={{8,0},{16,8},{24,16},{32,24},{40,32},{48,40},{56,48},{64,56},{72,6... | collective-permute-start | bytes 21512 | tf_op jit(solution)/shard_map/ppermute | solution.py:35
  109.2 1.0 fusion.87
  110.6 2.1 %gather_fusion.7 = f32[512,4,28]{2,1,0:T(4,128)S(1)} fusion(f32[4,28,576]{1,0,2:T(4,128)S(1)} %constant_dynamic-update-slice_fusion.15, s32[1024]{0:T(1024)S(1)} %copy-done.30), kind=kCustom, calls=%fused_computation.8.clone | custom fusion | bytes 460800 | tf_op jit(solution)/shard_map/jit(_take)/gather | solution.py:126
  118.1 1.0 fusion.88
  119.5 1.9 %collective-permute-start.16 = (f32[1,4,28,16]{2,1,3,0:T(4,128)S(1)}, f32[1,4,28,16]{2,1,3,0:T(4,128)S(1)}, u32[]{:S(2)}, u32[]{:S(2)}) collective-permute-start(f32[1,4,28,16]{2,1,3,0:T(4,128)S(1)} %get-tuple-element.16), channel_id=1, source_target_pairs={{0,1},{1,2},{2,3},{3,4},{4,5},{5,6},{6,7},{8,9},{9,10},{10,11},{11... | collective-permute-start | bytes 21512 | tf_op jit(solution)/shard_map/ppermute | solution.py:32
  121.7 5.1 %collective-permute-start.17 = (f32[1,4,28,16]{2,1,3,0:T(4,128)S(1)}, f32[1,4,28,16]{2,1,3,0:T(4,128)S(1)}, u32[]{:S(2)}, u32[]{:S(2)}) collective-permute-start(f32[1,4,28,16]{2,1,3,0:T(4,128)S(1)} %get-tuple-element.15), channel_id=1, source_target_pairs={{1,0},{2,1},{3,2},{4,3},{5,4},{6,5},{7,6},{9,8},{10,9},{11,10},{12... | collective-permute-start | bytes 21512 | tf_op jit(solution)/shard_map/ppermute | solution.py:35
  126.9 1.9 %collective-permute-start.18 = (f32[1,4,28,16]{2,1,3,0:T(4,128)S(1)}, f32[1,4,28,16]{2,1,3,0:T(4,128)S(1)}, u32[]{:S(2)}, u32[]{:S(2)}) collective-permute-start(f32[1,4,28,16]{2,1,3,0:T(4,128)S(1)} %get-tuple-element.14), channel_id=1, source_target_pairs={{0,8},{8,16},{16,24},{24,32},{32,40},{40,48},{48,56},{56,64},{64,7... | collective-permute-start | bytes 21512 | tf_op jit(solution)/shard_map/ppermute | solution.py:32
  128.8 5.8 %collective-permute-start.19 = (f32[1,4,28,16]{2,1,3,0:T(4,128)S(1)}, f32[1,4,28,16]{2,1,3,0:T(4,128)S(1)}, u32[]{:S(2)}, u32[]{:S(2)}) collective-permute-start(f32[1,4,28,16]{2,1,3,0:T(4,128)S(1)} %get-tuple-element.13), channel_id=1, source_target_pairs={{8,0},{16,8},{24,16},{32,24},{40,32},{48,40},{56,48},{64,56},{72,6... | collective-permute-start | bytes 21512 | tf_op jit(solution)/shard_map/ppermute | solution.py:35
  134.7 1.5 %collective-permute-done.19 = f32[1,4,28,16]{2,1,3,0:T(4,128)S(1)} collective-permute-done((f32[1,4,28,16]{2,1,3,0:T(4,128)S(1)}, f32[1,4,28,16]{2,1,3,0:T(4,128)S(1)}, u32[]{:S(2)}, u32[]{:S(2)}) %collective-permute-start.19) | collective-permute-done | bytes 7200 | tf_op jit(solution)/shard_map/ppermute | solution.py:35
  136.2 2.1 %gather_fusion.9 = f32[512,4,28]{2,1,0:T(4,128)S(1)} fusion(f32[4,28,576]{1,0,2:T(4,128)S(1)} %constant_dynamic-update-slice_fusion.20, s32[1024]{0:T(1024)S(1)} %copy-done.31), kind=kCustom, calls=%fused_computation.9.clone | custom fusion | bytes 460800 | tf_op jit(solution)/shard_map/jit(_take)/gather | solution.py:126
  139.7 0.9 fusion.49
  (297 shorter events, 26.8 us)
Async XLA Ops:
  0.0 29.3 %copy-start = (f32[3,84,84]{2,1,0:T(8,128)S(1)}, f32[3,84,84]{2,1,0:T(8,128)}, u32[]{:S(2)}) copy-start(f32[3,84,84]{2,1,0:T(8,128)} %param.16) | copy-start | bytes 254020
  3.4 10.5 %copy-start.32 = (s32[1024]{0:T(1024)}, s32[1024]{0:T(1024)S(1)}, u32[]{:S(2)}) copy-start(s32[1024]{0:T(1024)S(1)} %pad_clamp_fusion.1) | copy-start | bytes 12292
  4.2 23.6 %copy-start.52 = (s32[4,128]{1,0:T(4,128)S(1)}, s32[4,128]{1,0:T(4,128)}, u32[]{:S(2)}) copy-start(s32[4,128]{1,0:T(4,128)} %param.24) | copy-start | bytes 6148
  4.2 24.3 %copy-start.53 = (s32[4,128]{1,0:T(4,128)S(1)}, s32[4,128]{1,0:T(4,128)}, u32[]{:S(2)}) copy-start(s32[4,128]{1,0:T(4,128)} %param.25) | copy-start | bytes 6148
  4.2 24.8 %copy-start.54 = (f32[2,4,128]{2,1,0:T(4,128)S(1)}, f32[2,4,128]{2,1,0:T(4,128)}, u32[]{:S(2)}) copy-start(f32[2,4,128]{2,1,0:T(4,128)} %param.21) | copy-start | bytes 12292
  4.9 27.7 %collective-permute-start = (f32[1,4,28,16]{2,1,3,0:T(4,128)}, f32[1,4,28,16]{2,1,3,0:T(4,128)}, u32[]{:S(2)}, u32[]{:S(2)}) collective-permute-start(f32[1,4,28,16]{2,1,3,0:T(4,128)} %get-tuple-element.32), channel_id=1, source_target_pairs={{0,1},{1,2},{2,3},{3,4},{4,5},{5,6},{6,7},{8,9},{9,10},{10,11},{11... | collective-permute-start | bytes 21512 | tf_op jit(solution)/shard_map/ppermute | solution.py:32
  7.5 25.9 %collective-permute-start.1 = (f32[1,4,28,16]{2,1,3,0:T(4,128)}, f32[1,4,28,16]{2,1,3,0:T(4,128)}, u32[]{:S(2)}, u32[]{:S(2)}) collective-permute-start(f32[1,4,28,16]{2,1,3,0:T(4,128)} %get-tuple-element.31), channel_id=1, source_target_pairs={{1,0},{2,1},{3,2},{4,3},{5,4},{6,5},{7,6},{9,8},{10,9},{11,10},{12... | collective-permute-start | bytes 21512 | tf_op jit(solution)/shard_map/ppermute | solution.py:35
  11.9 22.2 %collective-permute-start.2 = (f32[1,4,28,16]{2,1,3,0:T(4,128)}, f32[1,4,28,16]{2,1,3,0:T(4,128)}, u32[]{:S(2)}, u32[]{:S(2)}) collective-permute-start(f32[1,4,28,16]{2,1,3,0:T(4,128)} %get-tuple-element.30), channel_id=1, source_target_pairs={{0,8},{8,16},{16,24},{24,32},{32,40},{40,48},{48,56},{56,64},{64,7... | collective-permute-start | bytes 21512 | tf_op jit(solution)/shard_map/ppermute | solution.py:32
  13.9 15.5 %copy-start.1 = (f32[4,84,128]{2,0,1:T(4,128)S(1)}, f32[4,84,128]{2,0,1:T(4,128)}, u32[]{:S(2)}) copy-start(f32[4,84,128]{2,0,1:T(4,128)} %param.15) | copy-start | bytes 516100
  13.9 21.0 %collective-permute-start.3 = (f32[1,4,28,16]{2,1,3,0:T(4,128)}, f32[1,4,28,16]{2,1,3,0:T(4,128)}, u32[]{:S(2)}, u32[]{:S(2)}) collective-permute-start(f32[1,4,28,16]{2,1,3,0:T(4,128)} %get-tuple-element.29), channel_id=1, source_target_pairs={{8,0},{16,8},{24,16},{32,24},{40,32},{48,40},{56,48},{64,56},{72,6... | collective-permute-start | bytes 21512 | tf_op jit(solution)/shard_map/ppermute | solution.py:35
  29.1 62.7 %copy-start.10 = (f32[3,4,128]{2,0,1:T(4,128)}, f32[3,4,128]{2,0,1:T(4,128)S(1)}, u32[]{:S(2)}) copy-start(f32[3,4,128]{2,0,1:T(4,128)S(1)} %copy.409) | copy-start | bytes 18436
  31.5 62.3 %copy-start.17 = (f32[128,3,3]{0,1,2:T(4,128)}, f32[128,3,3]{0,1,2:T(4,128)S(1)}, u32[]{:S(2)}) copy-start(f32[128,3,3]{0,1,2:T(4,128)S(1)} %copy.564) | copy-start | bytes 13828
  31.7 6.7 %copy-start.21 = (f32[4,128]{1,0:T(4,128)}, f32[4,128]{1,0:T(4,128)S(1)}, u32[]{:S(2)}) copy-start(f32[4,128]{1,0:T(4,128)S(1)} %select_reduce_fusion) | copy-start | bytes 6148
  31.7 6.0 %copy-start.27 = (s32[1024]{0:T(1024)}, s32[1024]{0:T(1024)S(1)}, u32[]{:S(2)}) copy-start(s32[1024]{0:T(1024)S(1)} %pad_clamp_fusion) | copy-start | bytes 12292
  31.8 6.3 %copy-start.47 = (pred[512]{0:T(512)(128)(4,1)S(1)}, pred[512]{0:T(512)(128)(4,1)}, u32[]{:S(2)}) copy-start(pred[512]{0:T(512)(128)(4,1)} %compare_and_fusion) | copy-start | bytes 1540
  32.5 80.7 %copy-start.8 = (f32[3,1,512]{2,0,1:T(4,128)}, f32[3,1,512]{2,0,1:T(4,128)S(1)}, u32[]{:S(2)}) copy-start(f32[3,1,512]{2,0,1:T(4,128)S(1)} %copy.610) | copy-start | bytes 18436
  32.5 81.1 %copy-start.6 = (f32[3,4,128]{2,0,1:T(4,128)}, f32[3,4,128]{2,0,1:T(4,128)S(1)}, u32[]{:S(2)}) copy-start(f32[3,4,128]{2,0,1:T(4,128)S(1)} %copy.413) | copy-start | bytes 18436
  35.6 2.8 %copy-start.37 = (pred[512]{0:T(512)(128)(4,1)S(1)}, pred[512]{0:T(512)(128)(4,1)}, u32[]{:S(2)}) copy-start(pred[512]{0:T(512)(128)(4,1)} %compare_bitcast_fusion) | copy-start | bytes 1540
  41.8 2.8 %copy-start.43 = (pred[4,16]{1,0:T(4,128)(4,1)S(1)}, pred[4,16]{1,0:T(4,128)(4,1)}, u32[]{:S(2)}) copy-start(pred[4,16]{1,0:T(4,128)(4,1)} %copy-done.42) | copy-start | bytes 196
  44.8 17.6 %collective-permute-start.4 = (f32[1,4,28,16]{2,1,3,0:T(4,128)S(1)}, f32[1,4,28,16]{2,1,3,0:T(4,128)S(1)}, u32[]{:S(2)}, u32[]{:S(2)}) collective-permute-start(f32[1,4,28,16]{2,1,3,0:T(4,128)S(1)} %get-tuple-element.28), channel_id=1, source_target_pairs={{0,1},{1,2},{2,3},{3,4},{4,5},{5,6},{6,7},{8,9},{9,10},{10,11},{11... | collective-permute-start | bytes 21512 | tf_op jit(solution)/shard_map/ppermute | solution.py:32
  46.7 15.7 %collective-permute-start.5 = (f32[1,4,28,16]{2,1,3,0:T(4,128)S(1)}, f32[1,4,28,16]{2,1,3,0:T(4,128)S(1)}, u32[]{:S(2)}, u32[]{:S(2)}) collective-permute-start(f32[1,4,28,16]{2,1,3,0:T(4,128)S(1)} %get-tuple-element.27), channel_id=1, source_target_pairs={{1,0},{2,1},{3,2},{4,3},{5,4},{6,5},{7,6},{9,8},{10,9},{11,10},{12... | collective-permute-start | bytes 21512 | tf_op jit(solution)/shard_map/ppermute | solution.py:35
  51.9 10.6 %collective-permute-start.6 = (f32[1,4,28,16]{2,1,3,0:T(4,128)S(1)}, f32[1,4,28,16]{2,1,3,0:T(4,128)S(1)}, u32[]{:S(2)}, u32[]{:S(2)}) collective-permute-start(f32[1,4,28,16]{2,1,3,0:T(4,128)S(1)} %get-tuple-element.26), channel_id=1, source_target_pairs={{0,8},{8,16},{16,24},{24,32},{32,40},{40,48},{48,56},{56,64},{64,7... | collective-permute-start | bytes 21512 | tf_op jit(solution)/shard_map/ppermute | solution.py:32
  53.8 8.7 %copy-start.28 = (s32[1024]{0:T(1024)S(1)}, s32[1024]{0:T(1024)}, u32[]{:S(2)}) copy-start(s32[1024]{0:T(1024)} %copy-done.27) | copy-start | bytes 12292
  53.8 8.7 %collective-permute-start.7 = (f32[1,4,28,16]{2,1,3,0:T(4,128)S(1)}, f32[1,4,28,16]{2,1,3,0:T(4,128)S(1)}, u32[]{:S(2)}, u32[]{:S(2)}) collective-permute-start(f32[1,4,28,16]{2,1,3,0:T(4,128)S(1)} %get-tuple-element.25), channel_id=1, source_target_pairs={{8,0},{16,8},{24,16},{32,24},{40,32},{48,40},{56,48},{64,56},{72,6... | collective-permute-start | bytes 21512 | tf_op jit(solution)/shard_map/ppermute | solution.py:35
  61.7 3.3 %copy-start.48 = (pred[512]{0:T(512)(128)(4,1)S(1)}, pred[512]{0:T(512)(128)(4,1)}, u32[]{:S(2)}) copy-start(pred[512]{0:T(512)(128)(4,1)} %compare_and_fusion) | copy-start | bytes 1540
  62.5 2.8 %copy-start.12 = (f32[1,28,4,128]{3,2,0,1:T(4,128)S(1)}, f32[1,28,4,128]{3,2,0,1:T(4,128)}, u32[]{:S(2)}) copy-start(f32[1,28,4,128]{3,2,0,1:T(4,128)} %copy.430) | copy-start | bytes 172036
  62.5 2.8 %copy-start.13 = (f32[28,4,128]{2,1,0:T(4,128)S(1)}, f32[28,4,128]{2,1,0:T(4,128)}, u32[]{:S(2)}) copy-start(f32[28,4,128]{2,1,0:T(4,128)} %copy.431) | copy-start | bytes 172036
  62.5 2.8 %copy-start.22 = (f32[4,128]{1,0:T(4,128)S(1)}, f32[4,128]{1,0:T(4,128)}, u32[]{:S(2)}) copy-start(f32[4,128]{1,0:T(4,128)} %copy-done.21) | copy-start | bytes 6148
  62.5 2.8 %copy-start.25 = (f32[4,128]{1,0:T(4,128)S(1)}, f32[4,128]{1,0:T(4,128)}, u32[]{:S(2)}) copy-start(f32[4,128]{1,0:T(4,128)} %param.20) | copy-start | bytes 6148
  62.5 2.8 %copy-start.38 = (pred[512]{0:T(512)(128)(4,1)S(1)}, pred[512]{0:T(512)(128)(4,1)}, u32[]{:S(2)}) copy-start(pred[512]{0:T(512)(128)(4,1)} %compare_bitcast_fusion) | copy-start | bytes 1540
  70.4 16.2 %collective-permute-start.8 = (f32[1,4,28,16]{2,1,3,0:T(4,128)S(1)}, f32[1,4,28,16]{2,1,3,0:T(4,128)S(1)}, u32[]{:S(2)}, u32[]{:S(2)}) collective-permute-start(f32[1,4,28,16]{2,1,3,0:T(4,128)S(1)} %get-tuple-element.24), channel_id=1, source_target_pairs={{0,1},{1,2},{2,3},{3,4},{4,5},{5,6},{6,7},{8,9},{9,10},{10,11},{11... | collective-permute-start | bytes 21512 | tf_op jit(solution)/shard_map/ppermute | solution.py:32
  72.3 14.3 %collective-permute-start.9 = (f32[1,4,28,16]{2,1,3,0:T(4,128)S(1)}, f32[1,4,28,16]{2,1,3,0:T(4,128)S(1)}, u32[]{:S(2)}, u32[]{:S(2)}) collective-permute-start(f32[1,4,28,16]{2,1,3,0:T(4,128)S(1)} %get-tuple-element.23), channel_id=1, source_target_pairs={{1,0},{2,1},{3,2},{4,3},{5,4},{6,5},{7,6},{9,8},{10,9},{11,10},{12... | collective-permute-start | bytes 21512 | tf_op jit(solution)/shard_map/ppermute | solution.py:35
  77.4 9.2 %collective-permute-start.10 = (f32[1,4,28,16]{2,1,3,0:T(4,128)S(1)}, f32[1,4,28,16]{2,1,3,0:T(4,128)S(1)}, u32[]{:S(2)}, u32[]{:S(2)}) collective-permute-start(f32[1,4,28,16]{2,1,3,0:T(4,128)S(1)} %get-tuple-element.22), channel_id=1, source_target_pairs={{0,8},{8,16},{16,24},{24,32},{32,40},{40,48},{48,56},{56,64},{64,7... | collective-permute-start | bytes 21512 | tf_op jit(solution)/shard_map/ppermute | solution.py:32
  79.4 7.4 %copy-start.29 = (s32[1024]{0:T(1024)S(1)}, s32[1024]{0:T(1024)}, u32[]{:S(2)}) copy-start(s32[1024]{0:T(1024)} %copy-done.27) | copy-start | bytes 12292
  79.4 7.3 %collective-permute-start.11 = (f32[1,4,28,16]{2,1,3,0:T(4,128)S(1)}, f32[1,4,28,16]{2,1,3,0:T(4,128)S(1)}, u32[]{:S(2)}, u32[]{:S(2)}) collective-permute-start(f32[1,4,28,16]{2,1,3,0:T(4,128)S(1)} %get-tuple-element.21), channel_id=1, source_target_pairs={{8,0},{16,8},{24,16},{32,24},{40,32},{48,40},{56,48},{64,56},{72,6... | collective-permute-start | bytes 21512 | tf_op jit(solution)/shard_map/ppermute | solution.py:35
  94.1 16.4 %collective-permute-start.12 = (f32[1,4,28,16]{2,1,3,0:T(4,128)S(1)}, f32[1,4,28,16]{2,1,3,0:T(4,128)S(1)}, u32[]{:S(2)}, u32[]{:S(2)}) collective-permute-start(f32[1,4,28,16]{2,1,3,0:T(4,128)S(1)} %get-tuple-element.20), channel_id=1, source_target_pairs={{0,1},{1,2},{2,3},{3,4},{4,5},{5,6},{6,7},{8,9},{9,10},{10,11},{11... | collective-permute-start | bytes 21512 | tf_op jit(solution)/shard_map/ppermute | solution.py:32
  96.0 14.5 %collective-permute-start.13 = (f32[1,4,28,16]{2,1,3,0:T(4,128)S(1)}, f32[1,4,28,16]{2,1,3,0:T(4,128)S(1)}, u32[]{:S(2)}, u32[]{:S(2)}) collective-permute-start(f32[1,4,28,16]{2,1,3,0:T(4,128)S(1)} %get-tuple-element.19), channel_id=1, source_target_pairs={{1,0},{2,1},{3,2},{4,3},{5,4},{6,5},{7,6},{9,8},{10,9},{11,10},{12... | collective-permute-start | bytes 21512 | tf_op jit(solution)/shard_map/ppermute | solution.py:35
  101.2 9.4 %collective-permute-start.14 = (f32[1,4,28,16]{2,1,3,0:T(4,128)S(1)}, f32[1,4,28,16]{2,1,3,0:T(4,128)S(1)}, u32[]{:S(2)}, u32[]{:S(2)}) collective-permute-start(f32[1,4,28,16]{2,1,3,0:T(4,128)S(1)} %get-tuple-element.18), channel_id=1, source_target_pairs={{0,8},{8,16},{16,24},{24,32},{32,40},{40,48},{48,56},{56,64},{64,7... | collective-permute-start | bytes 21512 | tf_op jit(solution)/shard_map/ppermute | solution.py:32
  103.1 7.5 %copy-start.30 = (s32[1024]{0:T(1024)S(1)}, s32[1024]{0:T(1024)}, u32[]{:S(2)}) copy-start(s32[1024]{0:T(1024)} %copy-done.27) | copy-start | bytes 12292
  103.1 7.5 %collective-permute-start.15 = (f32[1,4,28,16]{2,1,3,0:T(4,128)S(1)}, f32[1,4,28,16]{2,1,3,0:T(4,128)S(1)}, u32[]{:S(2)}, u32[]{:S(2)}) collective-permute-start(f32[1,4,28,16]{2,1,3,0:T(4,128)S(1)} %get-tuple-element.17), channel_id=1, source_target_pairs={{8,0},{16,8},{24,16},{32,24},{40,32},{48,40},{56,48},{64,56},{72,6... | collective-permute-start | bytes 21512 | tf_op jit(solution)/shard_map/ppermute | solution.py:35
  118.1 3.3 %copy-start.11 = (f32[3,4,128]{2,0,1:T(4,128)S(1)}, f32[3,4,128]{2,0,1:T(4,128)}, u32[]{:S(2)}) copy-start(f32[3,4,128]{2,0,1:T(4,128)} %copy-done.10) | copy-start | bytes 18436
  119.1 17.1 %copy-start.31 = (s32[1024]{0:T(1024)S(1)}, s32[1024]{0:T(1024)}, u32[]{:S(2)}) copy-start(s32[1024]{0:T(1024)} %copy-done.27) | copy-start | bytes 12292
  119.5 15.1 %collective-permute-start.16 = (f32[1,4,28,16]{2,1,3,0:T(4,128)S(1)}, f32[1,4,28,16]{2,1,3,0:T(4,128)S(1)}, u32[]{:S(2)}, u32[]{:S(2)}) collective-permute-start(f32[1,4,28,16]{2,1,3,0:T(4,128)S(1)} %get-tuple-element.16), channel_id=1, source_target_pairs={{0,1},{1,2},{2,3},{3,4},{4,5},{5,6},{6,7},{8,9},{9,10},{10,11},{11... | collective-permute-start | bytes 21512 | tf_op jit(solution)/shard_map/ppermute | solution.py:32
  121.6 17.0 %copy-start.51 = (pred[512]{0:T(512)(128)(4,1)S(1)}, pred[512]{0:T(512)(128)(4,1)}, u32[]{:S(2)}) copy-start(pred[512]{0:T(512)(128)(4,1)} %compare_and_fusion) | copy-start | bytes 1540
  121.7 12.9 %collective-permute-start.17 = (f32[1,4,28,16]{2,1,3,0:T(4,128)S(1)}, f32[1,4,28,16]{2,1,3,0:T(4,128)S(1)}, u32[]{:S(2)}, u32[]{:S(2)}) collective-permute-start(f32[1,4,28,16]{2,1,3,0:T(4,128)S(1)} %get-tuple-element.15), channel_id=1, source_target_pairs={{1,0},{2,1},{3,2},{4,3},{5,4},{6,5},{7,6},{9,8},{10,9},{11,10},{12... | collective-permute-start | bytes 21512 | tf_op jit(solution)/shard_map/ppermute | solution.py:35
  126.9 7.7 %collective-permute-start.18 = (f32[1,4,28,16]{2,1,3,0:T(4,128)S(1)}, f32[1,4,28,16]{2,1,3,0:T(4,128)S(1)}, u32[]{:S(2)}, u32[]{:S(2)}) collective-permute-start(f32[1,4,28,16]{2,1,3,0:T(4,128)S(1)} %get-tuple-element.14), channel_id=1, source_target_pairs={{0,8},{8,16},{16,24},{24,32},{32,40},{40,48},{48,56},{56,64},{64,7... | collective-permute-start | bytes 21512 | tf_op jit(solution)/shard_map/ppermute | solution.py:32
  128.8 7.3 %collective-permute-start.19 = (f32[1,4,28,16]{2,1,3,0:T(4,128)S(1)}, f32[1,4,28,16]{2,1,3,0:T(4,128)S(1)}, u32[]{:S(2)}, u32[]{:S(2)}) collective-permute-start(f32[1,4,28,16]{2,1,3,0:T(4,128)S(1)} %get-tuple-element.13), channel_id=1, source_target_pairs={{8,0},{16,8},{24,16},{32,24},{40,32},{48,40},{56,48},{64,56},{72,6... | collective-permute-start | bytes 21512 | tf_op jit(solution)/shard_map/ppermute | solution.py:35
  134.7 4.1 %copy-start.9 = (f32[3,1,512]{2,0,1:T(4,128)S(1)}, f32[3,1,512]{2,0,1:T(4,128)}, u32[]{:S(2)}) copy-start(f32[3,1,512]{2,0,1:T(4,128)} %copy-done.8) | copy-start | bytes 18436
  (28 other events, 48.0 us)
where the time goes:
time: 142 us; the launch traced here: 141 us
  starting transfers between devices  82.1 us (58%)
  local copies, waits for them, and re-layouts  31.3 us (22%)
  matrix products  12.4 us (9%)
  other arithmetic  11.1 us (8%)
  between operations  2.05 us (1%)
  waiting for transfers between devices  1.62 us (1%)
    ppermute x10, starting transfers between devices, extended(): lax.ppermute(lax.slice_in_dim(block, 0, width, axis=dim), axis, backward)  62.3 us
    ppermute x10, starting transfers between devices, extended(): lax.ppermute(lax.slice_in_dim(block, block.shape[dim] - width, None, axis...  19.9 us
    gather x10, local copies, waits for them, and re-layouts, shards(): neighbour = jnp.take(source_table, lookup, axis=2)  12.2 us
    unnamed x135, local copies, waits for them, and re-layouts  5.35 us
    dot_general x5, matrix products, tendency(): jnp.einsum('ace,ane->cne', inv_jacobian, slopes[:, 0], precision=HIGH)  4.93 us
    gather x5, local copies, waits for them, and re-layouts, shards(): packed = jnp.moveaxis(jnp.take(own_trace, send_list, axis=2), 2, 0)  3.28 us
    dot_general x5, matrix products, tendency(): slopes = jnp.einsum('anm,fme->afne', diff_ops, state_now, precision=HIGH)  2.95 us
    dot_general x5, matrix products, face_traces(): traces = jnp.einsum('jn,fne->fje', face_interp, state_now, precision=HIGH)  2.88 us
  transfers between devices with their start and end apart: 20, of which 2 were waited for; matrix products, arithmetic and copies ran while one was open for 9% of the time, Pallas kernels for 0%

commit v1 on v0

v1 whole, which is shorter than its diff:
```python
import functools

import jax
import jax.numpy as jnp
from jax import lax
from jax.experimental import pallas as pl
from jax.experimental.pallas import tpu as pltpu
from jax.sharding import PartitionSpec as P

MESH = pl.DeviceIdType.MESH
F32 = jnp.float32
BF16 = jnp.bfloat16
RK_A = (
    0.0,
    -567301805773.0 / 1357537059087.0,
    -2404267990393.0 / 2016746695238.0,
    -3550918686646.0 / 2091501179385.0,
    -1275806237668.0 / 842570457699.0,
)
RK_B = (
    1432997174477.0 / 9575080441755.0,
    5161836677717.0 / 13612068292357.0,
    1720146321549.0 / 2090206949498.0,
    3134564353537.0 / 4481467310338.0,
    2277821191437.0 / 14882151754819.0,
)
DT = 0.3
SECTIONS = 5
NP = 84
NR = 88
FR = 32
NFP = 28
ELEM = 128
FACES = 4 * ELEM
CAP = 16
SLOTS = 4 * CAP
BODY = 80


def iota(shape, dim):
    return lax.broadcasted_iota(jnp.int32, shape, dim)


def ones_where(cond):
    return jnp.where(cond, 1.0, 0.0).astype(BF16)


def halves(x):
    high = x.astype(BF16)
    return high, (x - high.astype(F32)).astype(BF16)


def mm(a, b):
    return jnp.dot(a, b, preferred_element_type=F32)


def mm_nt(a, b):
    return lax.dot_general(a, b, (((1,), (1,)), ((), ())), preferred_element_type=F32)


def spread_nodes():
    r, j = iota((NP, 256), 0), iota((NP, 256), 1)
    body = r < BODY
    high = (body & ((j == r) | (j == r + BODY))) | (~body & ((j == r + 160) | (j == r + 164)))
    low = (body & (j == r + 2 * BODY)) | (~body & (j == r + 168))
    return ones_where(high), ones_where(low)


def stack_state(q_ref, st_ref):
    for f in range(4):
        cols = slice(f * ELEM, (f + 1) * ELEM)
        high, low = halves(q_ref[f, 0:BODY, :])
        st_ref[0:BODY, cols] = high
        st_ref[BODY : 2 * BODY, cols] = low
        st_ref[2 * BODY : 3 * BODY, cols] = high
        tail = q_ref[f, BODY:NR, :]
        tail_high = tail.astype(BF16).astype(F32)
        tail_low = pltpu.roll(tail - tail_high, 4, 0)
        st_ref[3 * BODY : 256, cols] = jnp.concatenate([tail_high + tail_low, tail_high], axis=0).astype(BF16)


def kernel(
    n_group,
    n_sub,
    fields_hbm,
    diff_hbm,
    interp_hbm,
    lift_hbm,
    jac_hbm,
    scale_hbm,
    angle_hbm,
    reflect_hbm,
    send_hbm,
    recv_hbm,
    class_hbm,
    out_ref,
    fields,
    diff,
    interp,
    lift,
    jac,
    scale,
    angle,
    reflect,
    send,
    recv,
    klass,
    q,
    res,
    st,
    fpad,
    w_face,
    w_diff,
    w_lift,
    sel,
    oh_local,
    oh_far,
    coef,
    jcoef,
    own,
    table,
    upl,
    flux,
    send_buf,
    recv_buf,
    load_sem,
    send_sem,
    recv_sem,
):
    g, s = lax.axis_index("group"), lax.axis_index("sub")
    g_next, g_prev = lax.rem(g + 1, n_group), lax.rem(g + n_group - 1, n_group)
    s_next, s_prev = lax.rem(s + 1, n_sub), lax.rem(s + n_sub - 1, n_sub)
    peers = ((g, s_next), (g, s_prev), (g_next, s), (g_prev, s))

    loads = [
        pltpu.make_async_copy(src, dst, load_sem.at[i])
        for i, (src, dst) in enumerate(
            (
                (interp_hbm, interp),
                (fields_hbm, fields),
                (send_hbm, send),
                (recv_hbm, recv),
                (class_hbm, klass),
                (angle_hbm, angle),
                (scale_hbm, scale),
                (reflect_hbm, reflect),
                (jac_hbm, jac),
                (diff_hbm, diff),
                (lift_hbm, lift),
            )
        )
    ]
    for load in loads:
        load.start()
    barrier = pltpu.get_barrier_semaphore()
    for peer in peers:
        pl.semaphore_signal(barrier, inc=1, device_id=peer, device_id_type=MESH)

    spread_high, spread_low = spread_nodes()
    fpad[...] = jnp.zeros_like(fpad)
    loads[0].wait()
    for k in range(4):
        fpad[k * FR : k * FR + NFP, :] = interp[k * NFP : (k + 1) * NFP, :]
    high, low = halves(fpad[...])
    w_face[...] = (mm(high, spread_high) + mm(low, spread_low)).astype(BF16)
    loads[1].wait()
    for f in range(4):
        q[f, BODY:NR, :] = jnp.zeros((NR - BODY, ELEM), F32)
        q[f, 0:NP, :] = fields[f]
    stack_state(q, st)
    loads[2].wait()
    for j in range(4):
        wanted = jnp.transpose(jnp.broadcast_to(send[j : j + 1, :], (CAP, CAP)), (1, 0))[:, 0:1]
        sel[j * CAP : (j + 1) * CAP, :] = ones_where(iota((CAP, FACES), 1) == wanted)

    def copy_to(m, j):
        return pltpu.make_async_remote_copy(
            src_ref=send_buf.at[m, j],
            dst_ref=recv_buf.at[m, j],
            send_sem=send_sem.at[m, j],
            recv_sem=recv_sem.at[m, j],
            device_id=peers[j],
            device_id_type=MESH,
        )

    def face_part(m):
        traces = mm(w_face[...], st[...])
        for f in range(4):
            for k in range(4):
                block = traces[k * FR : (k + 1) * FR, f * ELEM : (f + 1) * ELEM]
                own[f, k] = block
                high, low = halves(block)
                table[f * FR : (f + 1) * FR, k * ELEM : (k + 1) * ELEM] = high
                table[4 * FR + f * FR : 4 * FR + (f + 1) * FR, k * ELEM : (k + 1) * ELEM] = low
        packed = mm_nt(sel[...], table[...])
        packed = packed[:, 0:128] + packed[:, 128:256]
        for j in range(4):
            send_buf[m, j] = packed[j * CAP : (j + 1) * CAP, :]

    def launch(m):
        for j in (2, 3, 0, 1):
            copy_to(m, j).start()

    def c8(i, k):
        return coef[i, k][None]

    def tile(x):
        return x.reshape(FR // 8, 8, ELEM)

    def local_part(m, a_now):
        vol = None
        for a in range(3):
            slopes = mm(w_diff[a], st[:, ELEM : 4 * ELEM])
            for c in range(3):
                term = slopes[:, c * ELEM : (c + 1) * ELEM].reshape(NR // 8, 8, ELEM) * jcoef[a, c][None]
                vol = term if vol is None else vol + term
        res[0] = a_now * res[0] + vol.reshape(NR, ELEM)
        slopes = [mm(w_diff[a], st[:, 0:ELEM]).reshape(NR // 8, 8, ELEM) for a in range(3)]
        for c in range(3):
            vol = sum(slopes[a] * jcoef[a, c][None] for a in range(3))
            res[1 + c] = a_now * res[1 + c] + vol.reshape(NR, ELEM)
        near = mm(table[...], oh_local[...])
        near = near[0:128, :] + near[128:256, :]
        for k in range(4):
            po, uo, vo, wo = (tile(own[f, k]) for f in range(4))
            pn, un, vn, wn = (
                tile(near[f * FR : (f + 1) * FR, k * ELEM : (k + 1) * ELEM]) for f in range(4)
            )
            nx, ny, nz, sc, rf = (c8(i, k) for i in range(5))
            minus = nx * uo + ny * vo + nz * wo
            got = pn + (nx * un + ny * vn + nz * wn)
            up = sc * (got + rf * (po - minus) - (po + minus))
            upl[k] = up.reshape(FR, ELEM)

    def far_part(m, b_now, last):
        arrived = recv_buf[m].reshape(SLOTS, 128)
        high = arrived.astype(BF16).astype(F32)
        both = jnp.concatenate([high, arrived - high], axis=0)
        far = mm(jnp.transpose(both, (1, 0)).astype(BF16), oh_far[...])
        for k in range(4):
            pn, un, vn, wn = (
                tile(far[f * FR : (f + 1) * FR, k * ELEM : (k + 1) * ELEM]) for f in range(4)
            )
            nx, ny, nz, sc = (c8(i, k) for i in range(4))
            up = tile(upl[k]) + sc * (pn + (nx * un + ny * vn + nz * wn))
            for f, term in enumerate((up, nx * up, ny * up, nz * up)):
                high, low = halves(term.reshape(FR, ELEM))
                flux[k * FR : (k + 1) * FR, f * ELEM : (f + 1) * ELEM] = high
                flux[4 * FR + k * FR : 4 * FR + (k + 1) * FR, f * ELEM : (f + 1) * ELEM] = low
        lifted = mm(w_lift[...], flux[...])
        lifted = lifted[0:NR, :] + lifted[NR : 2 * NR, :]
        for f in range(4):
            change = res[f] + lifted[:, f * ELEM : (f + 1) * ELEM]
            new = q[f] + b_now * change
            res[f] = change
            q[f] = new

    face_part(0)
    pl.semaphore_wait(barrier, 4)
    launch(0)

    for load in loads[3:]:
        load.wait()
    for k in range(4):
        rows = slice(k * ELEM, (k + 1) * ELEM)
        where = jnp.where(klass[k : k + 1, :] == 0, recv[k : k + 1, :], -1)
        oh_local[:, rows] = ones_where(iota((FACES, ELEM), 0) == where)
        slot = iota((2 * SLOTS, ELEM), 0)
        slot = jnp.where(slot >= SLOTS, slot - SLOTS, slot)
        oh_far[:, rows] = ones_where(slot + FACES == where)
        first, second = angle[0, k : k + 1, :], angle[1, k : k + 1, :]
        flat = jnp.cos(second)
        kinds = klass[k : k + 1, :]
        mirror = jnp.zeros((1, ELEM), F32)
        for c in range(4):
            mirror = mirror + jnp.where(kinds == c + 1, reflect[c], 0.0)
        for i, row in enumerate(
            (
                -(jnp.cos(first) * flat),
                -(jnp.sin(first) * flat),
                -jnp.sin(second),
                0.5 * scale[k : k + 1, :],
                mirror,
            )
        ):
            coef[i, k] = jnp.broadcast_to(row, (8, ELEM))
    for a in range(3):
        high, low = halves(diff[a] * (-DT))
        w_diff[a] = jnp.zeros((NR, 256), BF16)
        w_diff[a, 0:NP, :] = (mm(high, spread_high) + mm(low, spread_low)).astype(BF16)
        for c in range(3):
            jcoef[a, c] = jnp.broadcast_to(jac[a, c : c + 1, :], (8, ELEM))
    r, j = iota((4 * NFP, 4 * FR), 0), iota((4 * NFP, 4 * FR), 1)
    face = (r >= NFP).astype(jnp.int32) + (r >= 2 * NFP).astype(jnp.int32) + (r >= 3 * NFP).astype(jnp.int32)
    spread_face = ones_where(j == r + (FR - NFP) * face)
    high, low = halves(lift[...] * DT)
    high, low = mm(high, spread_face).astype(BF16), mm(low, spread_face).astype(BF16)
    w_lift[...] = jnp.zeros_like(w_lift)
    w_lift[0:NP, 0:128] = high
    w_lift[0:NP, 128:256] = high
    w_lift[NR : NR + NP, 0:128] = low
    for f in range(4):
        res[f] = jnp.zeros((NR, ELEM), F32)

    def finish(m, b_now):
        for j in range(4):
            copy_to(m, j).wait_recv()
        far_part(m, b_now, False)
        for j in range(4):
            copy_to(m, j).wait_send()

    def pick(values, m):
        out = jnp.float32(values[0])
        for i in range(1, SECTIONS):
            out = jnp.where(m == i, jnp.float32(values[i]), out)
        return out

    def section(m, carry):
        local_part(m - 1, pick(RK_A, m - 1))
        finish(m - 1, pick(RK_B, m - 1))
        stack_state(q, st)
        face_part(m)
        launch(m)
        return carry

    lax.fori_loop(1, SECTIONS, section, 0)
    local_part(SECTIONS - 1, RK_A[-1])
    finish(SECTIONS - 1, RK_B[-1])
    for f in range(4):
        out_ref[f] = q[f, 0:NP, :]


def shards(n_group, n_sub, *args):
    shapes = [a.shape for a in args]
    vm = pltpu.VMEM
    loaded = [
        pltpu.SMEM(x.shape, x.dtype) if i == 7 else vm(x.shape, x.dtype) for i, x in enumerate(args)
    ]
    return pl.pallas_call(
        functools.partial(kernel, n_group, n_sub),
        out_shape=jax.ShapeDtypeStruct(shapes[0], F32),
        in_specs=[pl.BlockSpec(memory_space=pl.ANY)] * len(args),
        out_specs=pl.BlockSpec(memory_space=pltpu.VMEM),
        scratch_shapes=loaded
        + [
            vm((4, NR, ELEM), F32),
            vm((4, NR, ELEM), F32),
            vm((256, FACES), BF16),
            vm((4 * FR, NP), F32),
            vm((4 * FR, 256), BF16),
            vm((3, NR, 256), BF16),
            vm((2 * NR, 256), BF16),
            vm((SLOTS, FACES), BF16),
            vm((FACES, FACES), BF16),
            vm((2 * SLOTS, FACES), BF16),
            vm((5, 4, 8, ELEM), F32),
            vm((3, 3, 8, ELEM), F32),
            vm((4, 4, FR, ELEM), F32),
            vm((256, FACES), BF16),
            vm((4, FR, ELEM), F32),
            vm((256, FACES), BF16),
            vm((SECTIONS, 4, CAP, 128), F32),
            vm((SECTIONS, 4, CAP, 128), F32),
            pltpu.SemaphoreType.DMA((len(args),)),
            pltpu.SemaphoreType.DMA((SECTIONS, 4)),
            pltpu.SemaphoreType.DMA((SECTIONS, 4)),
        ],
        compiler_params=pltpu.CompilerParams(collective_id=0, has_side_effects=True),
        name="sections",
    )(*args)


def solution(mesh):
    both = ("group", "sub")
    return jax.shard_map(
        functools.partial(shards, mesh.shape["group"], mesh.shape["sub"]),
        mesh=mesh,
        in_specs=(
            P(None, None, both),
            P(),
            P(),
            P(),
            P(None, None, both),
            P(None, both),
            P(None, None, both),
            P(),
            P(None, both),
            P(None, both),
            P(None, both),
        ),
        out_specs=P(None, None, both),
        check_vma=False,
    )
```

time: 142 us -> 45.5 us (0.32)
  the two profiles are of different devices: /device:TPU:38 before, /device:TPU:24 now
where the time goes in v1:
time: 45.5 us; the launch traced here: 45.3 us
  Pallas kernels  40.5 us (89%)
  local copies, waits for them, and re-layouts  4.73 us (10%)
    pallas_call x1, Pallas kernels, shards(): pl.pallas_call(functools.partial(kernel, n_group, n_sub), out_shape=jax.S...  40.5 us
    unnamed x2, local copies, waits for them, and re-layouts  3.1 us
    pallas_call x1, local copies, waits for them, and re-layouts, shards(): pl.pallas_call(functools.partial(kernel, n_group, n_sub), out_shape=jax.S...  1.64 us

profile of v1, /device:TPU:24, one launch (start us, length us, event | category | flops | bytes accessed | tf_op | source)
XLA Modules:
  0.0 45.3 jit_solution(2545108518379977379)
XLA Ops:
  0.0 1.5 %copy.13.interp_hbm = f32[112,84]{1,0:T(8,128)} copy(f32[112,84]{0,1:T(8,128)} %param.13) | data formatting | bytes 75264 | tf_op args[2]
  1.5 1.6 %copy.12.fields_hbm = f32[4,84,128]{2,1,0:T(8,128)} copy(f32[4,84,128]{2,0,1:T(4,128)} %param.11) | data formatting | bytes 344064 | tf_op args[0]
  3.1 40.5 %sections.1 = f32[4,84,128]{2,1,0:T(8,128)} custom-call(f32[4,84,128]{2,1,0:T(8,128)} %copy.12.fields_hbm, f32[3,84,84]{2,1,0:T(8,128)} %diff_hbm.1, f32[112,84]{1,0:T(8,128)} %copy.13.interp_hbm, f32[84,112]{1,0:T(8,128)} %lift_hbm.1, f32[3,3,128]{2,1,0:T(4,128)} %jac_hbm.1, f32[4,128]{1,0:T(4,128)} %scale_hbm.1, f32[2,4,128]{2,1,0:T(4,128)} %angle_hbm.1, ...), custom_call_target="tpu_custom_call" | custom-call | tf_op jit(solution)/shard_map/sections/pallas_call | solution.py:339
  43.6 1.6 %copy.14 = f32[4,84,128]{2,0,1:T(4,128)} copy(f32[4,84,128]{2,1,0:T(8,128)} %sections.1) | data formatting | bytes 344064 | tf_op jit(solution)/shard_map/sections/pallas_call | solution.py:339

commit v2 on v1

--- a/solution.py
+++ b/solution.py
@@ -130,6 +130,7 @@
     g, s = lax.axis_index("group"), lax.axis_index("sub")
     g_next, g_prev = lax.rem(g + 1, n_group), lax.rem(g + n_group - 1, n_group)
     s_next, s_prev = lax.rem(s + 1, n_sub), lax.rem(s + n_sub - 1, n_sub)
+    exists = (s < n_sub - 1, s > 0, g < n_group - 1, g > 0)
     peers = ((g, s_next), (g, s_prev), (g_next, s), (g_prev, s))
 
     loads = [
@@ -152,21 +153,27 @@
     ]
     for load in loads:
         load.start()
+    recv_buf[...] = jnp.zeros_like(recv_buf)
     barrier = pltpu.get_barrier_semaphore()
-    for peer in peers:
-        pl.semaphore_signal(barrier, inc=1, device_id=peer, device_id_type=MESH)
+    for peer, there in zip(peers, exists):
+
+        @pl.when(there)
+        def _(peer=peer):
+            pl.semaphore_signal(barrier, inc=1, device_id=peer, device_id_type=MESH)
+
 
     spread_high, spread_low = spread_nodes()
     fpad[...] = jnp.zeros_like(fpad)
     loads[0].wait()
+    rows = jnp.transpose(interp[...], (1, 0))
     for k in range(4):
-        fpad[k * FR : k * FR + NFP, :] = interp[k * NFP : (k + 1) * NFP, :]
+        fpad[k * FR : k * FR + NFP, :] = rows[k * NFP : (k + 1) * NFP, :]
     high, low = halves(fpad[...])
     w_face[...] = (mm(high, spread_high) + mm(low, spread_low)).astype(BF16)
     loads[1].wait()
     for f in range(4):
         q[f, BODY:NR, :] = jnp.zeros((NR - BODY, ELEM), F32)
-        q[f, 0:NP, :] = fields[f]
+        q[f, 0:NP, :] = fields[pl.ds(f, NP, stride=4), :]
     stack_state(q, st)
     loads[2].wait()
     for j in range(4):
@@ -199,7 +206,11 @@
 
     def launch(m):
         for j in (2, 3, 0, 1):
-            copy_to(m, j).start()
+
+            @pl.when(exists[j])
+            def _(j=j):
+                copy_to(m, j).start()
+
 
     def c8(i, k):
         return coef[i, k][None]
@@ -256,7 +267,7 @@
             q[f] = new
 
     face_part(0)
-    pl.semaphore_wait(barrier, 4)
+    pl.semaphore_wait(barrier, sum(e.astype(jnp.int32) for e in exists))
     launch(0)
 
     for load in loads[3:]:
@@ -303,11 +314,13 @@
         res[f] = jnp.zeros((NR, ELEM), F32)
 
     def finish(m, b_now):
-        for j in range(4):
-            copy_to(m, j).wait_recv()
+        for j in (0, 1, 2, 3):
+
+            @pl.when(exists[j ^ 1])
+            def _(j=j):
+                copy_to(m, j).wait_recv()
+
         far_part(m, b_now, False)
-        for j in range(4):
-            copy_to(m, j).wait_send()
 
     def pick(values, m):
         out = jnp.float32(values[0])
@@ -326,19 +339,27 @@
     lax.fori_loop(1, SECTIONS, section, 0)
     local_part(SECTIONS - 1, RK_A[-1])
     finish(SECTIONS - 1, RK_B[-1])
+    for j in range(4):
+
+        @pl.when(exists[j])
+        def _(j=j):
+            for m in range(SECTIONS):
+                copy_to(m, j).wait_send()
+
     for f in range(4):
-        out_ref[f] = q[f, 0:NP, :]
-
-
-def shards(n_group, n_sub, *args):
-    shapes = [a.shape for a in args]
+        out_ref[pl.ds(f, NP, stride=4), :] = q[f, 0:NP, :]
+
+
+def shards(n_group, n_sub, fields, diff_ops, face_interp, *rest):
+    rows = jnp.transpose(fields, (1, 0, 2)).reshape(4 * NP, ELEM)
+    args = (rows, diff_ops, jnp.transpose(face_interp, (1, 0))) + rest
     vm = pltpu.VMEM
     loaded = [
         pltpu.SMEM(x.shape, x.dtype) if i == 7 else vm(x.shape, x.dtype) for i, x in enumerate(args)
     ]
-    return pl.pallas_call(
+    out = pl.pallas_call(
         functools.partial(kernel, n_group, n_sub),
-        out_shape=jax.ShapeDtypeStruct(shapes[0], F32),
+        out_shape=jax.ShapeDtypeStruct(rows.shape, F32),
         in_specs=[pl.BlockSpec(memory_space=pl.ANY)] * len(args),
         out_specs=pl.BlockSpec(memory_space=pltpu.VMEM),
         scratch_shapes=loaded
@@ -368,6 +389,7 @@
         compiler_params=pltpu.CompilerParams(collective_id=0, has_side_effects=True),
         name="sections",
     )(*args)
+    return jnp.transpose(out.reshape(NP, 4, ELEM), (1, 0, 2))
 
 
 def solution(mesh):

time: 45.5 us -> 38 us (0.84)
  the two profiles are of different devices: /device:TPU:24 before, /device:TPU:30 now
where the time goes in v2:
time: 38 us; the launch traced here: 37.8 us
  Pallas kernels  36.2 us (95%)
  local copies, waits for them, and re-layouts  1.6 us (4%)
    pallas_call x1, Pallas kernels, shards(): pl.pallas_call(functools.partial(kernel, n_group, n_sub), out_shape=jax.S...  36.2 us
    unnamed x1, local copies, waits for them, and re-layouts  1.6 us

profile of v2, /device:TPU:30, one launch (start us, length us, event | category | flops | bytes accessed | tf_op | source)
XLA Modules:
  0.0 37.8 jit_solution(6441213117505972368)
XLA Ops:
  0.0 36.2 %sections.1 = f32[336,128]{1,0:T(8,128)} custom-call(f32[336,128]{1,0:T(8,128)} %bitcast.8, f32[3,84,84]{2,1,0:T(8,128)} %diff_hbm.1, f32[84,112]{1,0:T(8,128)} %bitcast.9, f32[84,112]{1,0:T(8,128)} %lift_hbm.1, f32[3,3,128]{2,1,0:T(4,128)} %jac_hbm.1, f32[4,128]{1,0:T(4,128)} %scale_hbm.1, f32[2,4,128]{2,1,0:T(4,128)} %angle_hbm.1, f32[4]{0:T(128)} %reflect_hbm.1, ...), custom_call_target="tpu_custom_call" | custom-call | tf_op jit(solution)/shard_map/sections/pallas_call | solution.py:360
  36.2 1.6 %copy.13 = f32[4,84,128]{2,0,1:T(4,128)} copy(f32[4,84,128]{2,0,1:T(4,128)} %bitcast.7) | data formatting | bytes 344064

commit v3 on v2

--- a/solution.py
+++ b/solution.py
@@ -350,6 +350,12 @@
         out_ref[pl.ds(f, NP, stride=4), :] = q[f, 0:NP, :]
 
 
+def hand_on(x_ref, out_ref, sem):
+    copy = pltpu.make_async_copy(x_ref, out_ref, sem)
+    copy.start()
+    copy.wait()
+
+
 def shards(n_group, n_sub, fields, diff_ops, face_interp, *rest):
     rows = jnp.transpose(fields, (1, 0, 2)).reshape(4 * NP, ELEM)
     args = (rows, diff_ops, jnp.transpose(face_interp, (1, 0))) + rest
@@ -357,6 +363,7 @@
     loaded = [
         pltpu.SMEM(x.shape, x.dtype) if i == 7 else vm(x.shape, x.dtype) for i, x in enumerate(args)
     ]
+    args = tuple(pltpu.with_memory_space_constraint(x, pltpu.HBM) for x in args)
     out = pl.pallas_call(
         functools.partial(kernel, n_group, n_sub),
         out_shape=jax.ShapeDtypeStruct(rows.shape, F32),
@@ -386,9 +393,20 @@
             pltpu.SemaphoreType.DMA((SECTIONS, 4)),
             pltpu.SemaphoreType.DMA((SECTIONS, 4)),
         ],
-        compiler_params=pltpu.CompilerParams(collective_id=0, has_side_effects=True),
+        compiler_params=pltpu.CompilerParams(
+            collective_id=0, has_side_effects=True, vmem_limit_bytes=16 << 20
+        ),
         name="sections",
     )(*args)
+    out = pl.pallas_call(
+        hand_on,
+        out_shape=jax.ShapeDtypeStruct(out.shape, F32),
+        in_specs=[pl.BlockSpec(memory_space=pltpu.VMEM)],
+        out_specs=pl.BlockSpec(memory_space=pl.ANY),
+        scratch_shapes=[pltpu.SemaphoreType.DMA],
+        compiler_params=pltpu.CompilerParams(vmem_limit_bytes=8 << 20),
+        name="hand_on",
+    )(out)
     return jnp.transpose(out.reshape(NP, 4, ELEM), (1, 0, 2))
 
 

time: 38 us -> 36.4 us (0.958)
  local copies, waits for them, and re-layouts: 1.6 us -> 0 us
    unnamed x1 -> x0, local copies, waits for them, and re-layouts: 1.6 us -> none
    pallas_call x0 -> x1, Pallas kernels: none -> 0.68 us  [shards(): pl.pallas_call(hand_on, out_shape=jax.ShapeDtypeStruct(out.shape, F32), i...]
    pallas_call x1, Pallas kernels: 36.2 us -> 35.6 us  [shards(): pl.pallas_call(functools.partial(kernel, n_group, n_sub), out_shape=jax.S...]
where the time goes in v3:
time: 36.4 us; the launch traced here: 36.2 us
  Pallas kernels  36.2 us (99%)
    pallas_call x1, Pallas kernels, shards(): pl.pallas_call(functools.partial(kernel, n_group, n_sub), out_shape=jax.S...  35.6 us

profile of v3, /device:TPU:30, one launch (start us, length us, event | category | flops | bytes accessed | tf_op | source)
XLA Modules:
  0.0 36.2 jit_solution(8471496755664504349)
XLA Ops:
  0.0 35.6 %sections.1.x_ref = f32[336,128]{1,0:T(8,128)S(1)} custom-call(f32[336,128]{1,0:T(8,128)} %bitcast.7, f32[3,84,84]{2,1,0:T(8,128)} %diff_hbm.1, f32[84,112]{1,0:T(8,128)} %bitcast.8, f32[84,112]{1,0:T(8,128)} %lift_hbm.1, f32[3,3,128]{2,1,0:T(4,128)} %jac_hbm.1, f32[4,128]{1,0:T(4,128)} %scale_hbm.1, f32[2,4,128]{2,1,0:T(4,128)} %angle_hbm.1, f32[4]{0:T(128)} %reflect_hbm.1, ...), custom_call_target="tpu_custom_call" | custom-call | tf_op jit(solution)/shard_map/sections/pallas_call | solution.py:367
  35.6 0.7 %hand_on.1 = f32[336,128]{1,0:T(8,128)} custom-call(f32[336,128]{1,0:T(8,128)S(1)} %sections.1.x_ref), custom_call_target="tpu_custom_call" | custom-call | tf_op jit(solution)/shard_map/hand_on/pallas_call | solution.py:401

commit v4 on v3

--- a/solution.py
+++ b/solution.py
@@ -66,17 +66,16 @@
     return ones_where(high), ones_where(low)
 
 
-def stack_state(q_ref, st_ref):
+def stack_state(q_ref):
+    columns = []
     for f in range(4):
-        cols = slice(f * ELEM, (f + 1) * ELEM)
         high, low = halves(q_ref[f, 0:BODY, :])
-        st_ref[0:BODY, cols] = high
-        st_ref[BODY : 2 * BODY, cols] = low
-        st_ref[2 * BODY : 3 * BODY, cols] = high
         tail = q_ref[f, BODY:NR, :]
         tail_high = tail.astype(BF16).astype(F32)
         tail_low = pltpu.roll(tail - tail_high, 4, 0)
-        st_ref[3 * BODY : 256, cols] = jnp.concatenate([tail_high + tail_low, tail_high], axis=0).astype(BF16)
+        tails = jnp.concatenate([tail_high + tail_low, tail_high], axis=0).astype(BF16)
+        columns.append(jnp.concatenate([high, low, high, tails], axis=0))
+    return jnp.concatenate(columns, axis=1)
 
 
 def kernel(
@@ -120,7 +119,6 @@
     own,
     table,
     upl,
-    flux,
     send_buf,
     recv_buf,
     load_sem,
@@ -174,7 +172,6 @@
     for f in range(4):
         q[f, BODY:NR, :] = jnp.zeros((NR - BODY, ELEM), F32)
         q[f, 0:NP, :] = fields[pl.ds(f, NP, stride=4), :]
-    stack_state(q, st)
     loads[2].wait()
     for j in range(4):
         wanted = jnp.transpose(jnp.broadcast_to(send[j : j + 1, :], (CAP, CAP)), (1, 0))[:, 0:1]
@@ -191,15 +188,25 @@
         )
 
     def face_part(m):
-        traces = mm(w_face[...], st[...])
+        state = stack_state(q)
+        traces = mm(w_face[...], state)
+        st[...] = state
+        blocks = {}
         for f in range(4):
             for k in range(4):
                 block = traces[k * FR : (k + 1) * FR, f * ELEM : (f + 1) * ELEM]
                 own[f, k] = block
-                high, low = halves(block)
-                table[f * FR : (f + 1) * FR, k * ELEM : (k + 1) * ELEM] = high
-                table[4 * FR + f * FR : 4 * FR + (f + 1) * FR, k * ELEM : (k + 1) * ELEM] = low
-        packed = mm_nt(sel[...], table[...])
+                blocks[0, f, k], blocks[1, f, k] = halves(block)
+        whole = jnp.concatenate(
+            [
+                jnp.concatenate([blocks[h, f, k] for k in range(4)], axis=1)
+                for h in range(2)
+                for f in range(4)
+            ],
+            axis=0,
+        )
+        packed = mm_nt(sel[...], whole)
+        table[...] = whole
         packed = packed[:, 0:128] + packed[:, 128:256]
         for j in range(4):
             send_buf[m, j] = packed[j * CAP : (j + 1) * CAP, :]
@@ -248,6 +255,7 @@
         high = arrived.astype(BF16).astype(F32)
         both = jnp.concatenate([high, arrived - high], axis=0)
         far = mm(jnp.transpose(both, (1, 0)).astype(BF16), oh_far[...])
+        parts = {}
         for k in range(4):
             pn, un, vn, wn = (
                 tile(far[f * FR : (f + 1) * FR, k * ELEM : (k + 1) * ELEM]) for f in range(4)
@@ -255,10 +263,16 @@
             nx, ny, nz, sc = (c8(i, k) for i in range(4))
             up = tile(upl[k]) + sc * (pn + (nx * un + ny * vn + nz * wn))
             for f, term in enumerate((up, nx * up, ny * up, nz * up)):
-                high, low = halves(term.reshape(FR, ELEM))
-                flux[k * FR : (k + 1) * FR, f * ELEM : (f + 1) * ELEM] = high
-                flux[4 * FR + k * FR : 4 * FR + (k + 1) * FR, f * ELEM : (f + 1) * ELEM] = low
-        lifted = mm(w_lift[...], flux[...])
+                parts[0, k, f], parts[1, k, f] = halves(term.reshape(FR, ELEM))
+        flux = jnp.concatenate(
+            [
+                jnp.concatenate([parts[h, k, f] for f in range(4)], axis=1)
+                for h in range(2)
+                for k in range(4)
+            ],
+            axis=0,
+        )
+        lifted = mm(w_lift[...], flux)
         lifted = lifted[0:NR, :] + lifted[NR : 2 * NR, :]
         for f in range(4):
             change = res[f] + lifted[:, f * ELEM : (f + 1) * ELEM]
@@ -331,7 +345,6 @@
     def section(m, carry):
         local_part(m - 1, pick(RK_A, m - 1))
         finish(m - 1, pick(RK_B, m - 1))
-        stack_state(q, st)
         face_part(m)
         launch(m)
         return carry
@@ -386,7 +399,6 @@
             vm((4, 4, FR, ELEM), F32),
             vm((256, FACES), BF16),
             vm((4, FR, ELEM), F32),
-            vm((256, FACES), BF16),
             vm((SECTIONS, 4, CAP, 128), F32),
             vm((SECTIONS, 4, CAP, 128), F32),
             pltpu.SemaphoreType.DMA((len(args),)),

time: 36.4 us -> 36 us (0.989)
  Pallas kernels: 36.2 us -> 35.8 us
    pallas_call x1, Pallas kernels: 35.6 us -> 35.2 us  [shards(): pl.pallas_call(functools.partial(kernel, n_group, n_sub), out_shape=jax.S...]
where the time goes in v4:
time: 36 us; the launch traced here: 35.9 us
  Pallas kernels  35.8 us (99%)
    pallas_call x1, Pallas kernels, shards(): pl.pallas_call(functools.partial(kernel, n_group, n_sub), out_shape=jax.S...  35.2 us

profile of v4, /device:TPU:30, one launch (start us, length us, event | category | flops | bytes accessed | tf_op | source)
XLA Modules:
  0.0 35.9 jit_solution(14338094751671657732)
XLA Ops:
  0.0 35.2 %sections.1.x_ref = f32[336,128]{1,0:T(8,128)S(1)} custom-call(f32[336,128]{1,0:T(8,128)} %bitcast.7, f32[3,84,84]{2,1,0:T(8,128)} %diff_hbm.1, f32[84,112]{1,0:T(8,128)} %bitcast.8, f32[84,112]{1,0:T(8,128)} %lift_hbm.1, f32[3,3,128]{2,1,0:T(4,128)} %jac_hbm.1, f32[4,128]{1,0:T(4,128)} %scale_hbm.1, f32[2,4,128]{2,1,0:T(4,128)} %angle_hbm.1, f32[4]{0:T(128)} %reflect_hbm.1, ...), custom_call_target="tpu_custom_call" | custom-call | tf_op jit(solution)/shard_map/sections/pallas_call | solution.py:380
  35.2 0.7 %hand_on.1 = f32[336,128]{1,0:T(8,128)} custom-call(f32[336,128]{1,0:T(8,128)S(1)} %sections.1.x_ref), custom_call_target="tpu_custom_call" | custom-call | tf_op jit(solution)/shard_map/hand_on/pallas_call | solution.py:413

commit v5 on v4

--- a/solution.py
+++ b/solution.py
@@ -34,6 +34,7 @@
 FACES = 4 * ELEM
 CAP = 16
 SLOTS = 4 * CAP
+POS = (0, 2, 1, 3)
 BODY = 80
 
 
@@ -116,9 +117,15 @@
     oh_far,
     coef,
     jcoef,
+    w_fl,
+    e_sel,
+    oh_sent,
+    sent_coef,
+    sent_flux,
+    sent_face,
+    base,
     own,
     table,
-    upl,
     send_buf,
     recv_buf,
     load_sem,
@@ -187,29 +194,37 @@
             device_id_type=MESH,
         )
 
-    def face_part(m):
-        state = stack_state(q)
+    def traces_of(state):
         traces = mm(w_face[...], state)
-        st[...] = state
-        blocks = {}
+        found, blocks = {}, {}
         for f in range(4):
             for k in range(4):
-                block = traces[k * FR : (k + 1) * FR, f * ELEM : (f + 1) * ELEM]
-                own[f, k] = block
-                blocks[0, f, k], blocks[1, f, k] = halves(block)
+                found[f, k] = traces[k * FR : (k + 1) * FR, f * ELEM : (f + 1) * ELEM]
+                blocks[0, f, k], blocks[1, f, k] = halves(found[f, k])
         whole = jnp.concatenate(
             [
                 jnp.concatenate([blocks[h, f, k] for k in range(4)], axis=1)
                 for h in range(2)
-                for f in range(4)
+                for f in POS
             ],
             axis=0,
         )
+        return found, whole
+
+    def keep(state, found, whole):
+        st[...] = state
+        table[...] = whole
+        for f in range(4):
+            for k in range(4):
+                own[f, k] = found[f, k]
+
+    def pack(whole):
         packed = mm_nt(sel[...], whole)
-        table[...] = whole
-        packed = packed[:, 0:128] + packed[:, 128:256]
+        return packed[:, 0:128] + packed[:, 128:256]
+
+    def send_rows(m, rows):
         for j in range(4):
-            send_buf[m, j] = packed[j * CAP : (j + 1) * CAP, :]
+            send_buf[m, j] = rows[j * CAP : (j + 1) * CAP, :]
 
     def launch(m):
         for j in (2, 3, 0, 1):
@@ -225,43 +240,14 @@
     def tile(x):
         return x.reshape(FR // 8, 8, ELEM)
 
-    def local_part(m, a_now):
-        vol = None
-        for a in range(3):
-            slopes = mm(w_diff[a], st[:, ELEM : 4 * ELEM])
-            for c in range(3):
-                term = slopes[:, c * ELEM : (c + 1) * ELEM].reshape(NR // 8, 8, ELEM) * jcoef[a, c][None]
-                vol = term if vol is None else vol + term
-        res[0] = a_now * res[0] + vol.reshape(NR, ELEM)
-        slopes = [mm(w_diff[a], st[:, 0:ELEM]).reshape(NR // 8, 8, ELEM) for a in range(3)]
-        for c in range(3):
-            vol = sum(slopes[a] * jcoef[a, c][None] for a in range(3))
-            res[1 + c] = a_now * res[1 + c] + vol.reshape(NR, ELEM)
-        near = mm(table[...], oh_local[...])
-        near = near[0:128, :] + near[128:256, :]
-        for k in range(4):
-            po, uo, vo, wo = (tile(own[f, k]) for f in range(4))
-            pn, un, vn, wn = (
-                tile(near[f * FR : (f + 1) * FR, k * ELEM : (k + 1) * ELEM]) for f in range(4)
-            )
-            nx, ny, nz, sc, rf = (c8(i, k) for i in range(5))
-            minus = nx * uo + ny * vo + nz * wo
-            got = pn + (nx * un + ny * vn + nz * wn)
-            up = sc * (got + rf * (po - minus) - (po + minus))
-            upl[k] = up.reshape(FR, ELEM)
-
-    def far_part(m, b_now, last):
-        arrived = recv_buf[m].reshape(SLOTS, 128)
-        high = arrived.astype(BF16).astype(F32)
-        both = jnp.concatenate([high, arrived - high], axis=0)
-        far = mm(jnp.transpose(both, (1, 0)).astype(BF16), oh_far[...])
+    def rows_of(array, f, k):
+        return tile(array[POS[f] * FR : (POS[f] + 1) * FR, k * ELEM : (k + 1) * ELEM])
+
+    def lift_up(ups):
         parts = {}
         for k in range(4):
-            pn, un, vn, wn = (
-                tile(far[f * FR : (f + 1) * FR, k * ELEM : (k + 1) * ELEM]) for f in range(4)
-            )
-            nx, ny, nz, sc = (c8(i, k) for i in range(4))
-            up = tile(upl[k]) + sc * (pn + (nx * un + ny * vn + nz * wn))
+            nx, ny, nz = (c8(i, k) for i in range(3))
+            up = ups[k]
             for f, term in enumerate((up, nx * up, ny * up, nz * up)):
                 parts[0, k, f], parts[1, k, f] = halves(term.reshape(FR, ELEM))
         flux = jnp.concatenate(
@@ -273,14 +259,89 @@
             axis=0,
         )
         lifted = mm(w_lift[...], flux)
-        lifted = lifted[0:NR, :] + lifted[NR : 2 * NR, :]
+        return lifted[0:NR, :] + lifted[NR : 2 * NR, :]
+
+    def local_part(a_now, b_now):
+        change = [None] * 4
+        vol = None
+        for a in range(3):
+            slopes = mm(w_diff[a], st[:, ELEM : 4 * ELEM])
+            for c in range(3):
+                term = slopes[:, c * ELEM : (c + 1) * ELEM].reshape(NR // 8, 8, ELEM) * jcoef[a, c][None]
+                vol = term if vol is None else vol + term
+        change[0] = a_now * res[0] + vol.reshape(NR, ELEM)
+        slopes = [mm(w_diff[a], st[:, 0:ELEM]).reshape(NR // 8, 8, ELEM) for a in range(3)]
+        for c in range(3):
+            vol = sum(slopes[a] * jcoef[a, c][None] for a in range(3))
+            change[1 + c] = a_now * res[1 + c] + vol.reshape(NR, ELEM)
+        near = mm(table[...], oh_local[...])
+        near = near[0:128, :] + near[128:256, :]
+        ups = []
+        for k in range(4):
+            po, uo, vo, wo = (tile(own[f, k]) for f in range(4))
+            pn, un, vn, wn = (rows_of(near, f, k) for f in range(4))
+            nx, ny, nz, sc, rf = (c8(i, k) for i in range(5))
+            minus = nx * uo + ny * vo + nz * wo
+            got = pn + (nx * un + ny * vn + nz * wn)
+            ups.append(sc * (got + rf * (po - minus) - (po + minus)))
+        lifted = lift_up(ups)
         for f in range(4):
-            change = res[f] + lifted[:, f * ELEM : (f + 1) * ELEM]
-            new = q[f] + b_now * change
-            res[f] = change
-            q[f] = new
-
-    face_part(0)
+            new = change[f] + lifted[:, f * ELEM : (f + 1) * ELEM]
+            res[f] = new
+            q[f] = q[f] + b_now * new
+
+    def received(m):
+        arrived = recv_buf[m].reshape(SLOTS, 128)
+        high = arrived.astype(BF16).astype(F32)
+        both = jnp.concatenate([high, arrived - high], axis=0)
+        return jnp.transpose(both, (1, 0)).astype(BF16)
+
+    def far_part(m, b_now):
+        far = mm(received(m), oh_far[...])
+        ups = []
+        for k in range(4):
+            pn, un, vn, wn = (rows_of(far, f, k) for f in range(4))
+            nx, ny, nz, sc = (c8(i, k) for i in range(4))
+            ups.append(sc * (pn + (nx * un + ny * vn + nz * wn)))
+        lifted = lift_up(ups)
+        for f in range(4):
+            more = lifted[:, f * ELEM : (f + 1) * ELEM]
+            res[f] = res[f] + more
+            q[f] = q[f] + b_now * more
+
+    def answer(m, b_now):
+        far = mm(received(m), oh_sent[...])
+        parts = {}
+        for k in range(4):
+            terms = [rows_of(far, f, k) * sent_coef[f, k][None] for f in range(4)]
+            up = (terms[0] + terms[1]) + (terms[2] + terms[3])
+            for p in range(2):
+                parts[0, k, p], parts[1, k, p] = halves((up * sent_flux[p, k][None]).reshape(FR, ELEM))
+        flux = jnp.concatenate(
+            [
+                jnp.concatenate([parts[h, k, p] for p in range(2)], axis=1)
+                for h in (0, 1, 0)
+                for k in range(4)
+            ],
+            axis=0,
+        )
+        moved = mm(w_fl[...], flux)
+        kept = []
+        for p in range(2):
+            kept.append(
+                sum(
+                    tile(moved[k * FR : (k + 1) * FR, p * ELEM : (p + 1) * ELEM]) * sent_face[k][None]
+                    for k in range(4)
+                ).reshape(FR, ELEM)
+            )
+        turned = jnp.transpose(jnp.concatenate(kept + kept, axis=0), (1, 0))
+        turned = jnp.where(iota((SLOTS, 128), 1) < SLOTS, turned[0:SLOTS, :], turned[SLOTS : 2 * SLOTS, :])
+        send_rows(m + 1, base[...] + b_now * turned)
+
+    state = stack_state(q)
+    found, whole = traces_of(state)
+    send_rows(0, pack(whole))
+    keep(state, found, whole)
     pl.semaphore_wait(barrier, sum(e.astype(jnp.int32) for e in exists))
     launch(0)
 
@@ -324,34 +385,62 @@
     w_lift[0:NP, 0:128] = high
     w_lift[0:NP, 128:256] = high
     w_lift[NR : NR + NP, 0:128] = low
+    f_high, f_low = halves(fpad[...])
+    both = mm(f_high, high) + (mm(f_high, low) + mm(f_low, high))
+    high, low = halves(both)
+    w_fl[:, 0:128] = high
+    w_fl[:, 128:256] = high
+    w_fl[:, 256:384] = low
+    picked = [sel[:, k * ELEM : (k + 1) * ELEM] for k in range(4)]
+    element = sum(x.astype(F32) for x in picked).astype(BF16)
+    e_sel[0:SLOTS, :] = element
+    e_sel[SLOTS : 2 * SLOTS, :] = element
+    upper = iota((8, ELEM), 1) < SLOTS
+    for k in range(4):
+        rows = slice(k * ELEM, (k + 1) * ELEM)
+        oh_sent[:, rows] = mm_nt(oh_far[:, rows], e_sel[...]).astype(BF16)
+        twice = jnp.concatenate([picked[k], picked[k]], axis=0)
+        sent_face[k] = mm_nt(jnp.ones((8, ELEM), BF16), twice)
+        nx, ny, nz, sc = (coef[i, k] for i in range(4))
+        high, low = halves(jnp.concatenate([nx, ny, nz, sc], axis=0))
+        there = mm_nt(high, e_sel[...]) + mm_nt(low, e_sel[...])
+        nx, ny, nz, sc = (there[i * 8 : (i + 1) * 8, :] for i in range(4))
+        for f, term in enumerate((sc, sc * nx, sc * ny, sc * nz)):
+            sent_coef[f, k] = term
+        sent_flux[0, k] = jnp.where(upper, 1.0, nx)
+        sent_flux[1, k] = jnp.where(upper, ny, nz)
     for f in range(4):
         res[f] = jnp.zeros((NR, ELEM), F32)
 
-    def finish(m, b_now):
+    def arrive(m):
         for j in (0, 1, 2, 3):
 
             @pl.when(exists[j ^ 1])
             def _(j=j):
                 copy_to(m, j).wait_recv()
 
-        far_part(m, b_now, False)
-
-    def pick(values, m):
+    def pick_of(values, m):
         out = jnp.float32(values[0])
         for i in range(1, SECTIONS):
             out = jnp.where(m == i, jnp.float32(values[i]), out)
         return out
 
     def section(m, carry):
-        local_part(m - 1, pick(RK_A, m - 1))
-        finish(m - 1, pick(RK_B, m - 1))
-        face_part(m)
-        launch(m)
+        a_now, b_now = pick_of(RK_A, m), pick_of(RK_B, m)
+        local_part(a_now, b_now)
+        base[...] = pack(traces_of(stack_state(q))[1])
+        arrive(m)
+        answer(m, b_now)
+        launch(m + 1)
+        far_part(m, b_now)
+        state = stack_state(q)
+        keep(state, *traces_of(state))
         return carry
 
-    lax.fori_loop(1, SECTIONS, section, 0)
-    local_part(SECTIONS - 1, RK_A[-1])
-    finish(SECTIONS - 1, RK_B[-1])
+    lax.fori_loop(0, SECTIONS - 1, section, 0)
+    local_part(RK_A[-1], RK_B[-1])
+    arrive(SECTIONS - 1)
+    far_part(SECTIONS - 1, RK_B[-1])
     for j in range(4):
 
         @pl.when(exists[j])
@@ -396,9 +485,15 @@
             vm((2 * SLOTS, FACES), BF16),
             vm((5, 4, 8, ELEM), F32),
             vm((3, 3, 8, ELEM), F32),
+            vm((4 * FR, 3 * 4 * FR), BF16),
+            vm((2 * SLOTS, ELEM), BF16),
+            vm((2 * SLOTS, FACES), BF16),
+            vm((4, 4, 8, ELEM), F32),
+            vm((2, 4, 8, ELEM), F32),
+            vm((4, 8, ELEM), F32),
+            vm((SLOTS, 128), F32),
             vm((4, 4, FR, ELEM), F32),
             vm((256, FACES), BF16),
-            vm((4, FR, ELEM), F32),
             vm((SECTIONS, 4, CAP, 128), F32),
             vm((SECTIONS, 4, CAP, 128), F32),
             pltpu.SemaphoreType.DMA((len(args),)),

time: 36 us -> 34.6 us (0.961)
  Pallas kernels: 35.8 us -> 34.5 us
    pallas_call x1, Pallas kernels: 35.2 us -> 33.8 us  [shards(): pl.pallas_call(functools.partial(kernel, n_group, n_sub), out_shape=jax.S...]
where the time goes in v5:
time: 34.6 us; the launch traced here: 34.5 us
  Pallas kernels  34.5 us (100%)
    pallas_call x1, Pallas kernels, shards(): pl.pallas_call(functools.partial(kernel, n_group, n_sub), out_shape=jax.S...  33.8 us

profile of v5, /device:TPU:30, one launch (start us, length us, event | category | flops | bytes accessed | tf_op | source)
XLA Modules:
  0.0 34.5 jit_solution(6659338431346272241)
XLA Ops:
  0.0 33.8 %sections.1.x_ref = f32[336,128]{1,0:T(8,128)S(1)} custom-call(f32[336,128]{1,0:T(8,128)} %bitcast.7, f32[3,84,84]{2,1,0:T(8,128)} %diff_hbm.1, f32[84,112]{1,0:T(8,128)} %bitcast.8, f32[84,112]{1,0:T(8,128)} %lift_hbm.1, f32[3,3,128]{2,1,0:T(4,128)} %jac_hbm.1, f32[4,128]{1,0:T(4,128)} %scale_hbm.1, f32[2,4,128]{2,1,0:T(4,128)} %angle_hbm.1, f32[4]{0:T(128)} %reflect_hbm.1, ...), custom_call_target="tpu_custom_call" | custom-call | tf_op jit(solution)/shard_map/sections/pallas_call | solution.py:469
  33.8 0.7 %hand_on.1 = f32[336,128]{1,0:T(8,128)} custom-call(f32[336,128]{1,0:T(8,128)S(1)} %sections.1.x_ref), custom_call_target="tpu_custom_call" | custom-call | tf_op jit(solution)/shard_map/hand_on/pallas_call | solution.py:508

commit v6 on v5

--- a/solution.py
+++ b/solution.py
@@ -156,9 +156,6 @@
             )
         )
     ]
-    for load in loads:
-        load.start()
-    recv_buf[...] = jnp.zeros_like(recv_buf)
     barrier = pltpu.get_barrier_semaphore()
     for peer, there in zip(peers, exists):
 
@@ -166,6 +163,14 @@
         def _(peer=peer):
             pl.semaphore_signal(barrier, inc=1, device_id=peer, device_id_type=MESH)
 
+    for load in loads:
+        load.start()
+    for j in range(4):
+
+        @pl.when(jnp.logical_not(exists[j ^ 1]))
+        def _(j=j):
+            for m in range(SECTIONS):
+                recv_buf[m, j] = jnp.zeros((CAP, 128), F32)
 
     spread_high, spread_low = spread_nodes()
     fpad[...] = jnp.zeros_like(fpad)
@@ -188,7 +193,7 @@
         return pltpu.make_async_remote_copy(
             src_ref=send_buf.at[m, j],
             dst_ref=recv_buf.at[m, j],
-            send_sem=send_sem.at[m, j],
+            send_sem=send_sem.at[j],
             recv_sem=recv_sem.at[m, j],
             device_id=peers[j],
             device_id_type=MESH,
@@ -227,7 +232,7 @@
             send_buf[m, j] = rows[j * CAP : (j + 1) * CAP, :]
 
     def launch(m):
-        for j in (2, 3, 0, 1):
+        for j in (0, 1, 2, 3):
 
             @pl.when(exists[j])
             def _(j=j):
@@ -419,6 +424,13 @@
             def _(j=j):
                 copy_to(m, j).wait_recv()
 
+    def sent(m):
+        for j in (0, 1, 2, 3):
+
+            @pl.when(exists[j])
+            def _(j=j):
+                copy_to(m, j).wait_send()
+
     def pick_of(values, m):
         out = jnp.float32(values[0])
         for i in range(1, SECTIONS):
@@ -429,6 +441,7 @@
         a_now, b_now = pick_of(RK_A, m), pick_of(RK_B, m)
         local_part(a_now, b_now)
         base[...] = pack(traces_of(stack_state(q))[1])
+        sent(m)
         arrive(m)
         answer(m, b_now)
         launch(m + 1)
@@ -439,15 +452,9 @@
 
     lax.fori_loop(0, SECTIONS - 1, section, 0)
     local_part(RK_A[-1], RK_B[-1])
+    sent(SECTIONS - 1)
     arrive(SECTIONS - 1)
     far_part(SECTIONS - 1, RK_B[-1])
-    for j in range(4):
-
-        @pl.when(exists[j])
-        def _(j=j):
-            for m in range(SECTIONS):
-                copy_to(m, j).wait_send()
-
     for f in range(4):
         out_ref[pl.ds(f, NP, stride=4), :] = q[f, 0:NP, :]
 
@@ -497,7 +504,7 @@
             vm((SECTIONS, 4, CAP, 128), F32),
             vm((SECTIONS, 4, CAP, 128), F32),
             pltpu.SemaphoreType.DMA((len(args),)),
-            pltpu.SemaphoreType.DMA((SECTIONS, 4)),
+            pltpu.SemaphoreType.DMA((4,)),
             pltpu.SemaphoreType.DMA((SECTIONS, 4)),
         ],
         compiler_params=pltpu.CompilerParams(

time: 34.6 us -> 34.5 us (level)
  no operation moved by 1% of the time
where the time goes in v6:
time: 34.5 us; the launch traced here: 34.3 us
  Pallas kernels  34.3 us (99%)
    pallas_call x1, Pallas kernels, shards(): pl.pallas_call(functools.partial(kernel, n_group, n_sub), out_shape=jax.S...  33.6 us

profile of v6, /device:TPU:30, one launch (start us, length us, event | category | flops | bytes accessed | tf_op | source)
XLA Modules:
  0.0 34.3 jit_solution(8447874542982922663)
XLA Ops:
  0.0 33.6 %sections.1.x_ref = f32[336,128]{1,0:T(8,128)S(1)} custom-call(f32[336,128]{1,0:T(8,128)} %bitcast.7, f32[3,84,84]{2,1,0:T(8,128)} %diff_hbm.1, f32[84,112]{1,0:T(8,128)} %bitcast.8, f32[84,112]{1,0:T(8,128)} %lift_hbm.1, f32[3,3,128]{2,1,0:T(4,128)} %jac_hbm.1, f32[4,128]{1,0:T(4,128)} %scale_hbm.1, f32[2,4,128]{2,1,0:T(4,128)} %angle_hbm.1, f32[4]{0:T(128)} %reflect_hbm.1, ...), custom_call_target="tpu_custom_call" | custom-call | tf_op jit(solution)/shard_map/sections/pallas_call | solution.py:476
  33.7 0.7 %hand_on.1 = f32[336,128]{1,0:T(8,128)} custom-call(f32[336,128]{1,0:T(8,128)S(1)} %sections.1.x_ref), custom_call_target="tpu_custom_call" | custom-call | tf_op jit(solution)/shard_map/hand_on/pallas_call | solution.py:515

commit v7 on v6

--- a/solution.py
+++ b/solution.py
@@ -194,7 +194,7 @@
             src_ref=send_buf.at[m, j],
             dst_ref=recv_buf.at[m, j],
             send_sem=send_sem.at[j],
-            recv_sem=recv_sem.at[m, j],
+            recv_sem=recv_sem.at[lax.rem(m, 2) if not isinstance(m, int) else m % 2, j],
             device_id=peers[j],
             device_id_type=MESH,
         )
@@ -301,7 +301,7 @@
         both = jnp.concatenate([high, arrived - high], axis=0)
         return jnp.transpose(both, (1, 0)).astype(BF16)
 
-    def far_part(m, b_now):
+    def far_part(m, b_now, last=False):
         far = mm(received(m), oh_far[...])
         ups = []
         for k in range(4):
@@ -311,6 +311,9 @@
         lifted = lift_up(ups)
         for f in range(4):
             more = lifted[:, f * ELEM : (f + 1) * ELEM]
+            if last:
+                out_ref[pl.ds(f, NP, stride=4), :] = q[f, 0:NP, :] + b_now * more[0:NP, :]
+                continue
             res[f] = res[f] + more
             q[f] = q[f] + b_now * more
 
@@ -454,9 +457,7 @@
     local_part(RK_A[-1], RK_B[-1])
     sent(SECTIONS - 1)
     arrive(SECTIONS - 1)
-    far_part(SECTIONS - 1, RK_B[-1])
-    for f in range(4):
-        out_ref[pl.ds(f, NP, stride=4), :] = q[f, 0:NP, :]
+    far_part(SECTIONS - 1, RK_B[-1], last=True)
 
 
 def hand_on(x_ref, out_ref, sem):
@@ -505,7 +506,7 @@
             vm((SECTIONS, 4, CAP, 128), F32),
             pltpu.SemaphoreType.DMA((len(args),)),
             pltpu.SemaphoreType.DMA((4,)),
-            pltpu.SemaphoreType.DMA((SECTIONS, 4)),
+            pltpu.SemaphoreType.DMA((2, 4)),
         ],
         compiler_params=pltpu.CompilerParams(
             collective_id=0, has_side_effects=True, vmem_limit_bytes=16 << 20

time: 34.5 us -> 34.4 us (level)
  no operation moved by 1% of the time
where the time goes in v7:
time: 34.4 us; the launch traced here: 34.2 us
  Pallas kernels  34.2 us (99%)
    pallas_call x1, Pallas kernels, shards(): pl.pallas_call(functools.partial(kernel, n_group, n_sub), out_shape=jax.S...  33.5 us

profile of v7, /device:TPU:30, one launch (start us, length us, event | category | flops | bytes accessed | tf_op | source)
XLA Modules:
  0.0 34.2 jit_solution(12012711102841624090)
XLA Ops:
  0.0 33.5 %sections.1.x_ref = f32[336,128]{1,0:T(8,128)S(1)} custom-call(f32[336,128]{1,0:T(8,128)} %bitcast.7, f32[3,84,84]{2,1,0:T(8,128)} %diff_hbm.1, f32[84,112]{1,0:T(8,128)} %bitcast.8, f32[84,112]{1,0:T(8,128)} %lift_hbm.1, f32[3,3,128]{2,1,0:T(4,128)} %jac_hbm.1, f32[4,128]{1,0:T(4,128)} %scale_hbm.1, f32[2,4,128]{2,1,0:T(4,128)} %angle_hbm.1, f32[4]{0:T(128)} %reflect_hbm.1, ...), custom_call_target="tpu_custom_call" | custom-call | tf_op jit(solution)/shard_map/sections/pallas_call | solution.py:477
  33.5 0.7 %hand_on.1 = f32[336,128]{1,0:T(8,128)} custom-call(f32[336,128]{1,0:T(8,128)S(1)} %sections.1.x_ref), custom_call_target="tpu_custom_call" | custom-call | tf_op jit(solution)/shard_map/hand_on/pallas_call | solution.py:516
